TPU v7x, 32 devices: a whole 2x2x4 slice. The times are simulated.
32 devices in a mesh: gx: 16 (over z, y, x), gy: 2 (over core).
Axes of the slice: x: 2, y: 2, z: 4, core: 2. Of those that a mesh axis runs over, the one named last changes fastest.
Arguments:
- density: float32 [128, 32, 64], P('gx', None, 'gy'), may hold values from 0.5 to 1.5
- momentum: float32 [3, 128, 32, 64], P(None, 'gx', None, 'gy'), may hold values from -3 to 3
- energy: float32 [128, 32, 64], P('gx', None, 'gy'), may hold values from 2.5 to 4
- eddy_normal_cell: int32 [1024], P('gx'), may hold values from 0 to 63
- eddy_spanwise_cell: int32 [1024], P('gx'), may hold values from 0 to 31
- eddy_signs: int32 [1024, 3], P('gx'), may hold values from 0 to 1
- eddy_strengths: float32 [1024], P('gx'), may hold values from 0.3 to 3
- filter_matrices: float32 [1, 128, 128], replicated, may hold values from -1.25 to 1.25
- shock_switch: int32 [1, 64], P(None, 'gy'), may hold values 0 or 1
- dilatation_bin: int32 [128, 32, 64], P('gx', None, 'gy'), may hold values from 0 to 63
- vorticity_bin: int32 [128, 32, 64], P('gx', None, 'gy'), may hold values from 0 to 63, as said below
Outputs:
- conserved_next: float32 [5, 128, 32, 64], P(None, 'gx', None, 'gy')
- histogram: float32 [64, 64], replicated
Inputs may be any that keep to these rules, and one draw needn't show every extreme that they name: vorticity_bin at streamwise cell x is x * 64 // 128 or one more, modulo 64.
All inputs are finite; a program needn't handle non-finite values. No bound on the sum of `shock_switch` on one device may be relied on, other than what follows from the above.
Results may differ from a plain program's by a relative error of at most 0.0003.
Values sent between devices are 32-bit elements; how exact they have to be, the bound alone decides.
No kernel may reach another device: no remote copies, remote signals or barrier semaphores. Data moves between devices by JAX's collectives and lax.ppermute only.
A program may use at most 64 MiB of HBM per device.

v0:
```python
import math

import jax
import jax.numpy as jnp
from jax import lax
from jax.sharding import PartitionSpec as P

HISTOGRAM_BINS = 64
SIGMA_Y = 32
SIGMA_Z = 8


TIME_STEP = 0.1
GAMMA_GAS = 1.4
SENSOR_EPS = 0.1
HAT_PEAK = math.sqrt(1.5)


def extended(x, sides, width):
    for axis, dim in sides:
        size, length = (lax.axis_size(axis), x.shape[dim])
        up = [(i, (i + 1) % size) for i in range(size - 1)]
        down = [(j, i) for i, j in up]
        last = lax.slice_in_dim(x, length - width, length, axis=dim)
        first = lax.slice_in_dim(x, 0, width, axis=dim)
        before = lax.ppermute(last, axis, up)
        after = lax.ppermute(first, axis, down)
        x = jnp.concatenate([before, x, after], axis=dim)
    return x


def hat_shape(centres, coords, spread, period):
    offset = coords[None, :] - centres[:, None]
    if period > 0:
        offset = jnp.mod(offset + period / 2, period) - period / 2
    return HAT_PEAK * jnp.maximum(0.0, 1.0 - jnp.abs(offset) / spread)


def inflow_from(centre_y, centre_z, eddy_weight, coords_y, coords_z, span):
    shape_y = hat_shape(centre_y, coords_y, float(SIGMA_Y), 0)
    shape_z = hat_shape(centre_z, coords_z, float(SIGMA_Z), span)
    weighted = (eddy_weight[:, :, None] * shape_z[:, None, :]).reshape(eddy_weight.shape[0], -1)
    inflow = jnp.dot(weighted.T, shape_y, precision=lax.Precision.HIGHEST)
    return inflow.reshape(3, coords_z.shape[0], coords_y.shape[0])


def ghost_state(inflow):
    mom_x = 1.0 + inflow[0]
    kinetic = mom_x * mom_x + inflow[1] * inflow[1] + inflow[2] * inflow[2]
    return jnp.stack([jnp.ones_like(mom_x), mom_x, inflow[1], inflow[2], 3.0 + 0.5 * kinetic])


def flux_of(fields, velocity, pressure, direction):
    result = fields * velocity[direction][None]
    result = result.at[1 + direction].add(pressure)
    return result.at[4].add(pressure * velocity[direction])


def central_x(values):
    return (values[..., 2:, :, 1:-1] - values[..., :-2, :, 1:-1]) * 0.5


def central_y(values):
    return (values[..., 1:-1, :, 2:] - values[..., 1:-1, :, :-2]) * 0.5


def central_z(values):
    centre = values[..., 1:-1, :, 1:-1]
    return (jnp.roll(centre, -1, axis=-2) - jnp.roll(centre, 1, axis=-2)) * 0.5


def section_rhs(padded):
    velocity = padded[1:4] / padded[0][None]
    pressure = (GAMMA_GAS - 1.0) * (padded[4] - 0.5 * jnp.sum(padded[1:4] * velocity, axis=0))
    change = central_x(flux_of(padded, velocity, pressure, 0))
    change = change + central_y(flux_of(padded, velocity, pressure, 1))
    change = change + central_z(flux_of(padded, velocity, pressure, 2))
    updated = padded[:, 1:-1, :, 1:-1] - TIME_STEP * change
    dilatation = central_x(velocity[0]) + central_y(velocity[1]) + central_z(velocity[2])
    vort_x = central_y(velocity[2]) - central_z(velocity[1])
    vort_y = central_z(velocity[0]) - central_x(velocity[2])
    vort_z = central_x(velocity[1]) - central_y(velocity[0])
    squared = dilatation * dilatation
    shock_sensor = squared / (
        squared + vort_x * vort_x + vort_y * vort_y + vort_z * vort_z + SENSOR_EPS
    )
    return (updated, shock_sensor)


def filter_lines(pencil, filter_matrices):
    block_count, block_len = (filter_matrices.shape[0], filter_matrices.shape[1])
    lanes = pencil.shape[2]
    blocks = pencil.reshape(5, block_count, block_len, lanes)
    smooth = jnp.einsum("bij,fbjp->fbip", filter_matrices, blocks, precision=lax.Precision.HIGHEST)
    return smooth.reshape(5, block_count * block_len, lanes)


def plane_histogram(shock_sensor, dilatation_bin, vorticity_bin):
    bin_levels = jnp.arange(HISTOGRAM_BINS, dtype=jnp.int32)

    def accumulate_plane(histogram_totals, histogram_parts):
        sensor_plane, plane_dilatation, plane_vorticity = histogram_parts
        flat_sensor = sensor_plane.reshape(-1)
        dilatation_table = (plane_dilatation.reshape(-1)[None, :] == bin_levels[:, None]).astype(
            jnp.float32
        )
        vorticity_table = jnp.where(
            plane_vorticity.reshape(-1)[:, None] == bin_levels[None, :], flat_sensor[:, None], 0.0
        )
        return (
            histogram_totals
            + jnp.dot(dilatation_table, vorticity_table, precision=lax.Precision.HIGHEST),
            None,
        )

    histogram_totals, _ = lax.scan(
        accumulate_plane,
        jnp.zeros((HISTOGRAM_BINS, HISTOGRAM_BINS), jnp.float32),
        (shock_sensor, dilatation_bin, vorticity_bin),
    )
    return histogram_totals


def shards(
    density,
    momentum,
    energy,
    eddy_normal_cell,
    eddy_spanwise_cell,
    eddy_signs,
    eddy_strengths,
    filter_matrices,
    shock_switch,
    dilatation_bin,
    vorticity_bin,
):
    cells_x, span, cells_y = density.shape
    slab_index = lax.axis_index("gx")
    block_index = lax.axis_index("gy")
    slab_count = lax.axis_size("gx")
    fields = jnp.concatenate([density[None], momentum, energy[None]], axis=0)
    total_y = cells_y * lax.axis_size("gy")
    total_eddies = eddy_normal_cell.shape[0] * slab_count
    amplitude = math.sqrt(total_y * span / (total_eddies * SIGMA_Y * SIGMA_Z))
    eddy_weight = (2 * eddy_signs - 1).astype(jnp.float32) * eddy_strengths[:, None] * amplitude
    coords_y = (block_index * cells_y + jnp.arange(cells_y, dtype=jnp.int32)).astype(jnp.float32)
    coords_z = jnp.arange(span, dtype=jnp.int32).astype(jnp.float32)
    partial_sum = inflow_from(
        eddy_normal_cell.astype(jnp.float32),
        eddy_spanwise_cell.astype(jnp.float32),
        eddy_weight,
        coords_y,
        coords_z,
        span,
    )
    inflow = lax.psum(partial_sum, "gx")
    ghost_cells = ghost_state(inflow)
    padded = extended(fields, (("gx", 1), ("gy", 3)), 1)
    padded = padded.at[:, 0, :, 1:-1].set(
        jnp.where(slab_index == 0, ghost_cells, padded[:, 0, :, 1:-1])
    )
    padded = padded.at[:, -1, :, 1:-1].set(
        jnp.where(slab_index == slab_count - 1, fields[:, -1], padded[:, -1, :, 1:-1])
    )
    padded = padded.at[:, 1:-1, :, 0].set(
        jnp.where(block_index == 0, fields[:, :, :, 0], padded[:, 1:-1, :, 0])
    )
    padded = padded.at[:, 1:-1, :, -1].set(
        jnp.where(
            block_index == lax.axis_size("gy") - 1, fields[:, :, :, -1], padded[:, 1:-1, :, -1]
        )
    )
    updated, shock_sensor = section_rhs(padded)
    block_len = filter_matrices.shape[1]
    filter_row = slab_index * cells_x // block_len
    mask_row = lax.dynamic_slice_in_dim(shock_switch, filter_row, 1, 0).astype(jnp.float32)
    weight = mask_row[None] * shock_sensor
    columns = span * cells_y
    stacked = updated.reshape(5, cells_x, columns)
    weight_flat = weight.reshape(1, cells_x, columns)
    pencil, pencil_weight = (
        lax.all_to_all(stacked, "gx", split_axis=2, concat_axis=1, tiled=True),
        lax.all_to_all(weight_flat, "gx", split_axis=2, concat_axis=1, tiled=True),
    )
    smooth = filter_lines(pencil, filter_matrices)
    returned = pencil + pencil_weight * (smooth - pencil)
    back_lines = lax.all_to_all(returned, "gx", split_axis=1, concat_axis=2, tiled=True)
    conserved_next = back_lines.reshape(5, cells_x, span, cells_y)
    partial_histogram = plane_histogram(shock_sensor, dilatation_bin, vorticity_bin)
    summed = lax.psum(partial_histogram, ("gx", "gy"))
    all_cells = cells_x * slab_count * span * total_y
    histogram = summed * (HISTOGRAM_BINS * HISTOGRAM_BINS / all_cells)
    return (conserved_next, histogram)


def solution(mesh):
    in_specs = (
        P("gx", None, "gy"),
        P(None, "gx", None, "gy"),
        P("gx", None, "gy"),
        P("gx"),
        P("gx"),
        P("gx", None),
        P("gx"),
        P(),
        P(None, "gy"),
        P("gx", None, "gy"),
        P("gx", None, "gy"),
    )
    out_specs = (P(None, "gx", None, "gy"), P())
    return jax.shard_map(shards, mesh=mesh, in_specs=in_specs, out_specs=out_specs, check_vma=False)
```

profile of v0, /device:TPU:0, one launch (start us, length us, event | category | flops | bytes accessed | tf_op | source)
XLA Modules:
  0.0 215.9 jit_solution(9551707045615207745)
XLA Ops:
  1.6 1.3 collective-permute-start.1
  2.9 5.5 %collective-permute-start = (f32[5,1,32,32]{3,2,0,1:T(8,128)S(1)}, f32[5,1,32,32]{3,2,0,1:T(8,128)S(1)}, u32[]{:S(2)}, u32[]{:S(2)}) collective-permute-start(f32[5,1,32,32]{3,2,0,1:T(8,128)S(1)} %get-tuple-element.222), channel_id=1, source_target_pairs={{0,2},{2,4},{4,6},{6,8},{8,10},{10,12},{12,14},{14,16},{16,18},{18... | collective-permute-start | bytes 61448 | tf_op jit(solution)/shard_map/ppermute | solution.py:26
  10.8 75.6 %psum.14 = f32[3,32,32]{2,1,0:T(8,128)S(1)} all-reduce(f32[3,32,32]{2,1,0:T(8,128)S(1)} %fusion.50), channel_id=1, replica_groups=mesh['gx'=16,'gy'=2] {'gx'}, use_global_device_ids=true, to_apply=%region_1.2 | all-reduce | flops 3072 | bytes 24576 | tf_op jit(solution)/shard_map/psum | solution.py:156
  91.2 1.3 collective-permute-start.3
  92.5 3.0 %collective-permute-start.2 = (f32[5,10,32,1]{2,3,1,0:T(1,128)S(1)}, f32[5,10,32,1]{2,3,1,0:T(1,128)S(1)}, u32[]{:S(2)}, u32[]{:S(2)}) collective-permute-start(f32[5,10,32,1]{2,3,1,0:T(1,128)S(1)} %copy.81), channel_id=1, source_target_pairs={{0,1},{2,3},{4,5},{6,7},{8,9},{10,11},{12,13},{14,15},{16,17},{18,... | collective-permute-start | bytes 19208 | tf_op jit(solution)/shard_map/ppermute | solution.py:26
  95.5 1.4 and_reduce_fusion
  97.3 1.3 copy.84
  98.6 1.6 pad_maximum_fusion.1
  100.2 1.4 fusion.48
  101.6 1.7 scatter.14
  105.9 3.7 %scatter.19 = f32[5,10,32,34]{3,2,0,1:T(8,128)S(1)} dynamic-update-slice(f32[5,10,32,34]{3,2,0,1:T(8,128)S(1)} %scatter.16, f32[5,8,32,1]{3,2,0,1:T(8,128)S(1)} %slice_select_fusion, s32[]{:T(128)} %constant.328.clone.1, s32[]{:T(128)} %constant.350.clone.1, s32[]{:T(128)} %constant.328.clone.1, s32[]{:T(128)} %constant.351.clone.1) | dynamic-update-slice | bytes 10244 | tf_op jit(solution)/shard_map/scatter | solution.py:168
  114.4 3.7 %reduce.27 = f32[1024,8]{1,0:T(8,128)} reduce(f32[1024,1,8]{2,1,0:T(1,128)} %bitcast.128, f32[]{:T(128)} %broadcast.273), dimensions={1}, to_apply=%bitcast.110.reduce_sub_computation | reduce | bytes 65540
  118.1 1.9 reshape.467
  120.0 3.5 %all-to-all-start.1 = ((f32[16,1,512]{2,1,0:T(1,128)}), f32[16,1,512]{2,1,0:T(1,128)S(1)}, u32[]{:S(2)}, u32[]{:S(2)}) async-start(f32[16,1,512]{2,1,0:T(1,128)} %reshape.467), calls=%async_computation.1 | async-start | bytes 65536 | tf_op jit(solution)/shard_map/all_to_all | solution.py:183
  123.5 2.7 %fusion.14 = f32[5,8,32,32]{3,2,0,1:T(8,128)} fusion(f32[5,10,32,34]{3,2,0,1:T(8,128)S(1)} %get-tuple-element.221, f32[5,10,32,34]{3,2,0,1:T(8,128)S(1)} %scatter.19, f32[5,8,1,32]{3,2,0,1:T(1,128)S(1)} %get-tuple-element.213, f32[5,8,31,32]{3,2,0,1:T(8,128)} %get-tuple-element.215, f32[5,8,31,32]{3,2,0,1:T(8,128)S(1)} %get-tuple-element.214, ...), kind=kLoop, calls=%fused_computation.23 | loop fusion | flops 368640 | bytes 4295680 | tf_op jit(solution)/shard_map/sub | solution.py:78
  126.2 3.6 %copy.122 = f32[5,8,32,32]{1,0,3,2:T(8,128)} copy(f32[5,8,32,32]{3,2,0,1:T(8,128)} %fusion.14) | data formatting | bytes 327680 | tf_op jit(solution)/shard_map/reshape | solution.py:179
  129.8 3.4 %reshape.465 = f32[16,1,2560]{2,1,0:T(1,128)} reshape(f32[1024,5,8]{2,1,0:T(8,128)} %bitcast.117) | data formatting | bytes 327680
  133.1 6.9 %all-to-all-start = ((f32[16,1,2560]{2,1,0:T(1,128)}), f32[16,1,2560]{2,1,0:T(1,128)S(1)}, u32[]{:S(2)}, u32[]{:S(2)}) async-start(f32[16,1,2560]{2,1,0:T(1,128)} %reshape.465), calls=%async_computation | async-start | bytes 327680 | tf_op jit(solution)/shard_map/all_to_all | solution.py:182
  141.8 6.1 %all-to-all-done = f32[16,1,2560]{2,1,0:T(1,128)S(1)} async-done(((f32[16,1,2560]{2,1,0:T(1,128)}), f32[16,1,2560]{2,1,0:T(1,128)S(1)}, u32[]{:S(2)}, u32[]{:S(2)}) %all-to-all-start) | async-done | bytes 163872 | tf_op jit(solution)/shard_map/all_to_all | solution.py:182
  148.9 2.6 %reshape.466 = f32[1024,5,8]{2,1,0:T(8,128)} reshape(f32[16,2560]{1,0:T(8,128)S(1)} %reduce.26) | data formatting | bytes 327680
  151.5 2.6 %copy.103 = f32[5,16,8,64]{3,2,1,0:T(8,128)S(1)} copy(f32[5,16,8,64]{2,0,3,1:T(8,128)} %bitcast.118) | data formatting | bytes 327680 | tf_op jit(solution)/shard_map/all_to_all | solution.py:182
  156.1 3.5 %all-to-all-start.2 = ((f32[16,1,2560]{2,1,0:T(1,128)}), f32[16,1,2560]{2,1,0:T(1,128)S(1)}, u32[]{:S(2)}, u32[]{:S(2)}) async-start(f32[16,1,2560]{2,1,0:T(1,128)} %reshape.469), calls=%async_computation.2 | async-start | bytes 327680 | tf_op jit(solution)/shard_map/all_to_all | solution.py:187
  159.6 12.6 %while.22 = (s32[]{:T(128)}, f32[64,64]{1,0:T(8,128)S(1)}, s32[8,32,32]{2,1,0:T(8,128)}, s32[8,32,32]{2,1,0:T(8,128)}, f32[8,32,32]{2,1,0:T(8,128)S(1)}, /*index=5*/s32[]{:T(128)}, s32[]{:T(128)}) while((s32[]{:T(128)}, f32[64,64]{1,0:T(8,128)S(1)}, s32[8,32,32]{2,1,0:T(8,128)}, s32[8,32,32]{2,1,0:T(8,128)}, ...), condition=%wide.region_4.5_spmd.clone.clone, body=%wide.region_3.4_spmd.clone.clone.sunk | while | flops 50536448 | bytes 94311 | solution.py:116
  172.2 40.8 %psum.15 = f32[64,64]{1,0:T(8,128)S(1)} all-reduce(f32[64,64]{1,0:T(8,128)S(1)} %get-tuple-element.157), channel_id=1, replica_groups=mesh['gx'=16,'gy'=2] {'gx','gy'}, use_global_device_ids=true, to_apply=%region_5.6 | all-reduce | flops 4096 | bytes 32768 | tf_op jit(solution)/shard_map/psum | solution.py:190
  (125 shorter events, 35.6 us)
Async XLA Ops:
  0.6 153.6 %copy-start = (f32[1,128,128]{2,1,0:T(8,128)S(1)}, f32[1,128,128]{2,1,0:T(8,128)}, u32[]{:S(2)}) copy-start(f32[1,128,128]{2,1,0:T(8,128)} %param.40) | copy-start | bytes 196612
  1.6 93.9 %copy-start.4 = (s32[4]{0:T(128)S(1)}, s32[4]{0:T(128)}, u32[]{:S(2)}) copy-start(s32[4]{0:T(128)} %constant.330.clone.1) | copy-start | bytes 52
  1.6 87.3 %collective-permute-start.1 = (f32[5,1,32,32]{3,2,0,1:T(8,128)S(1)}, f32[5,1,32,32]{3,2,0,1:T(8,128)S(1)}, u32[]{:S(2)}, u32[]{:S(2)}) collective-permute-start(f32[5,1,32,32]{3,2,0,1:T(8,128)S(1)} %get-tuple-element.223), channel_id=1, source_target_pairs={{2,0},{4,2},{6,4},{8,6},{10,8},{12,10},{14,12},{16,14},{18,16},{20... | collective-permute-start | bytes 61448 | tf_op jit(solution)/shard_map/ppermute | solution.py:27
  2.9 86.0 %collective-permute-start = (f32[5,1,32,32]{3,2,0,1:T(8,128)S(1)}, f32[5,1,32,32]{3,2,0,1:T(8,128)S(1)}, u32[]{:S(2)}, u32[]{:S(2)}) collective-permute-start(f32[5,1,32,32]{3,2,0,1:T(8,128)S(1)} %get-tuple-element.222), channel_id=1, source_target_pairs={{0,2},{2,4},{4,6},{6,8},{8,10},{10,12},{12,14},{14,16},{16,18},{18... | collective-permute-start | bytes 61448 | tf_op jit(solution)/shard_map/ppermute | solution.py:26
  87.6 11.0 %copy-start.1 = (f32[3,8,32,32]{3,2,1,0:T(8,128)S(1)}, f32[3,8,32,32]{3,2,1,0:T(8,128)}, u32[]{:S(2)}) copy-start(f32[3,8,32,32]{3,2,1,0:T(8,128)} %param.34) | copy-start | bytes 294916
  87.6 11.0 %copy-start.2 = (f32[8,32,32]{2,1,0:T(8,128)S(1)}, f32[8,32,32]{2,1,0:T(8,128)}, u32[]{:S(2)}) copy-start(f32[8,32,32]{2,1,0:T(8,128)} %param.35) | copy-start | bytes 98308
  87.6 11.0 %copy-start.3 = (f32[8,32,32]{2,1,0:T(8,128)S(1)}, f32[8,32,32]{2,1,0:T(8,128)}, u32[]{:S(2)}) copy-start(f32[8,32,32]{2,1,0:T(8,128)} %param.33) | copy-start | bytes 98308
  91.2 6.1 %collective-permute-start.3 = (f32[5,10,32,1]{2,3,1,0:T(1,128)S(1)}, f32[5,10,32,1]{2,3,1,0:T(1,128)S(1)}, u32[]{:S(2)}, u32[]{:S(2)}) collective-permute-start(f32[5,10,32,1]{2,3,1,0:T(1,128)S(1)} %copy.82), channel_id=1, source_target_pairs={{1,0},{3,2},{5,4},{7,6},{9,8},{11,10},{13,12},{15,14},{17,16},{19,... | collective-permute-start | bytes 19208 | tf_op jit(solution)/shard_map/ppermute | solution.py:27
  92.5 4.4 %collective-permute-start.2 = (f32[5,10,32,1]{2,3,1,0:T(1,128)S(1)}, f32[5,10,32,1]{2,3,1,0:T(1,128)S(1)}, u32[]{:S(2)}, u32[]{:S(2)}) collective-permute-start(f32[5,10,32,1]{2,3,1,0:T(1,128)S(1)} %copy.81), channel_id=1, source_target_pairs={{0,1},{2,3},{4,5},{6,7},{8,9},{10,11},{12,13},{14,15},{16,17},{18,... | collective-permute-start | bytes 19208 | tf_op jit(solution)/shard_map/ppermute | solution.py:26
  120.0 13.2 %all-to-all-start.1 = ((f32[16,1,512]{2,1,0:T(1,128)}), f32[16,1,512]{2,1,0:T(1,128)S(1)}, u32[]{:S(2)}, u32[]{:S(2)}) async-start(f32[16,1,512]{2,1,0:T(1,128)} %reshape.467), calls=%async_computation.1 | async-start | bytes 65536 | tf_op jit(solution)/shard_map/all_to_all | solution.py:183
  133.1 14.8 %all-to-all-start = ((f32[16,1,2560]{2,1,0:T(1,128)}), f32[16,1,2560]{2,1,0:T(1,128)S(1)}, u32[]{:S(2)}, u32[]{:S(2)}) async-start(f32[16,1,2560]{2,1,0:T(1,128)} %reshape.465), calls=%async_computation | async-start | bytes 327680 | tf_op jit(solution)/shard_map/all_to_all | solution.py:182
  156.1 57.5 %all-to-all-start.2 = ((f32[16,1,2560]{2,1,0:T(1,128)}), f32[16,1,2560]{2,1,0:T(1,128)S(1)}, u32[]{:S(2)}, u32[]{:S(2)}) async-start(f32[16,1,2560]{2,1,0:T(1,128)} %reshape.469), calls=%async_computation.2 | async-start | bytes 327680 | tf_op jit(solution)/shard_map/all_to_all | solution.py:187
where the time goes:
time: 218 us; the launch traced here: 216 us
  blocking collectives  116 us (53%)
  local copies, waits for them, and re-layouts  39.7 us (18%)
  starting transfers between devices  25 us (11%)
  other arithmetic  21.8 us (10%)
  waiting for transfers between devices  6.13 us (3%)
  matrix products  5.55 us (3%)
    psum x1, blocking collectives, shards(): inflow = lax.psum(partial_sum, 'gx')  75.6 us
    psum x1, blocking collectives, shards(): summed = lax.psum(partial_histogram, ('gx', 'gy'))  40.8 us
    unnamed x16, local copies, waits for them, and re-layouts  9.82 us
    ppermute x2, starting transfers between devices, extended(): before = lax.ppermute(last, axis, up)  8.5 us
    all_to_all x1, starting transfers between devices, shards(): lax.all_to_all(stacked, 'gx', split_axis=2, concat_axis=1, tiled=True)  6.88 us
    all_to_all x1, waiting for transfers between devices, shards(): lax.all_to_all(stacked, 'gx', split_axis=2, concat_axis=1, tiled=True)  6.11 us
    dynamic_slice x16, local copies, waits for them, and re-layouts, plane_histogram(): lax.scan(accumulate_plane, jnp.zeros((HISTOGRAM_BINS, HISTOGRAM_BINS), jn...  6 us
    dot_general x8, matrix products, accumulate_plane(): jnp.dot(dilatation_table, vorticity_table, precision=lax.Precision.HIGHEST)  4.61 us
  transfers between devices with their start and end apart: 7, of which 1 were waited for; matrix products, arithmetic and copies ran while one was open for 14% of the time, Pallas kernels for 0%

commit v1 on v0

--- a/solution.py
+++ b/solution.py
@@ -3,6 +3,8 @@
 import jax
 import jax.numpy as jnp
 from jax import lax
+from jax.experimental import pallas as pl
+from jax.experimental.pallas import tpu as pltpu
 from jax.sharding import PartitionSpec as P
 
 HISTOGRAM_BINS = 64
@@ -121,7 +123,7 @@
     return histogram_totals
 
 
-def shards(
+def general_shards(
     density,
     momentum,
     energy,
@@ -193,6 +195,478 @@
     return (conserved_next, histogram)
 
 
+LANES = 128
+HALF_STEP = 0.5 * TIME_STEP
+
+
+def iota(shape, dim):
+    return lax.broadcasted_iota(jnp.int32, shape, dim)
+
+
+def roll(x, shift, axis):
+    shift %= x.shape[axis]
+    return x if shift == 0 else pltpu.roll(x, shift, axis)
+
+
+def packed(ref, *lead):
+    parts = [ref[(*lead, slice(None), pl.ds(8 * k, 8), slice(None))] for k in range(4)]
+    return jnp.concatenate(parts, axis=-1)
+
+
+def regrouped(parts, k):
+    group = iota(parts[0].shape, len(parts[0].shape) - 1) // 32
+    out = None
+    for i, part in enumerate(parts):
+        moved = roll(part, 32 * (i - k), len(part.shape) - 1)
+        out = moved if out is None else jnp.where(group == i, moved, out)
+    return out
+
+
+def velocity_pressure(q):
+    inverse = 1.0 / q[0]
+    vel = [q[1] * inverse, q[2] * inverse, q[3] * inverse]
+    kinetic = q[1] * vel[0] + q[2] * vel[1] + q[3] * vel[2]
+    return vel, (GAMMA_GAS - 1.0) * (q[4] - 0.5 * kinetic)
+
+
+def euler_flux(q, vel, pressure, k):
+    flux = [q[1 + k], q[1] * vel[k], q[2] * vel[k], q[3] * vel[k], (q[4] + pressure) * vel[k]]
+    flux[1 + k] = flux[1 + k] + pressure
+    return flux
+
+
+def z_difference(a):
+    row = iota(a.shape, 1)
+    up = roll(a, -1, 1)
+    up = jnp.where(row == 7, roll(up, -32, 2), up)
+    down = roll(a, 1, 1)
+    down = jnp.where(row == 0, roll(down, 32, 2), down)
+    return up - down
+
+
+def y_difference(a, first_core):
+    lane = iota(a.shape, 2) % 32
+    up = jnp.where(lane == 31, jnp.where(first_core, 0.0, a), roll(a, -1, 2))
+    down = jnp.where(lane == 0, jnp.where(first_core, a, 0.0), roll(a, 1, 2))
+    return up - down
+
+
+def x_difference(a, before, after):
+    up = jnp.concatenate([a[1:], after], axis=0)
+    down = jnp.concatenate([before, a[:-1]], axis=0)
+    return up - down
+
+
+def slab_kernel(
+    amplitude,
+    density,
+    momentum,
+    energy,
+    normal_cell,
+    spanwise_cell,
+    signs,
+    strengths,
+    send,
+    partial_out,
+    velocity_out,
+    first_out,
+    last_out,
+    edge_out,
+):
+    slab = lax.axis_index("gx")
+    first_core = lax.axis_index("gy") == 0
+    last_slab = slab == lax.axis_size("gx") - 1
+    q = [packed(density)] + [packed(momentum, c) for c in range(3)] + [packed(energy)]
+    vel, pressure = velocity_pressure(q)
+    flux_x = euler_flux(q, vel, pressure, 0)
+    flux_y = euler_flux(q, vel, pressure, 1)
+    flux_z = euler_flux(q, vel, pressure, 2)
+    zero = jnp.zeros((1, 8, LANES), jnp.float32)
+    partial = []
+    for f in range(5):
+        after = jnp.where(last_slab, flux_x[f][7:], 0.0)
+        change = x_difference(flux_x[f], zero, after)
+        change = change + y_difference(flux_y[f], first_core)
+        change = change + z_difference(flux_z[f])
+        partial.append(q[f] - HALF_STEP * change)
+        partial_out[f] = partial[f]
+        first_out[f] = q[f][0]
+        last_out[f] = q[f][7]
+    for c in range(3):
+        velocity_out[c] = vel[c]
+
+    lane = iota((8, 8, LANES), 2) % 32
+    edge = jnp.zeros((8, 8, LANES), jnp.float32)
+    for i, value in enumerate(flux_y + vel):
+        near = jnp.where(first_core, roll(value, i - 31, 2), roll(value, i, 2))
+        edge = jnp.where(lane == i, near, edge)
+    edge_out[...] = edge
+
+    own = slice(0, 32), slice(32, 64)
+    pick = lambda a: jnp.where(first_core, a[:, own[0]], a[:, own[1]])
+    strength = strengths[...] * amplitude
+    rows = [pick(normal_cell[...]).astype(jnp.float32), pick(spanwise_cell[...]).astype(jnp.float32)]
+    for c in range(3):
+        sign = (2 * signs[c : c + 1, :] - 1).astype(jnp.float32)
+        rows.append(pick(sign * strength))
+    blank = jnp.zeros((1, 32), jnp.float32)
+    eddies = jnp.concatenate([blank] + rows + [blank, blank], axis=0)
+    eddies = jnp.concatenate([eddies] * 4, axis=1)
+
+    slots = [flux_x[4][7], None, None, None, None, None, None, flux_x[4][0]]
+    extra = jnp.stack([eddies if s is None else s for s in slots])
+    faces = [None] * 8
+    for f in range(4):
+        faces[2 * f] = flux_x[f][7]
+        faces[(2 * f - 1) % 8] = flux_x[f][0]
+    faces = jnp.stack(faces)
+    row = iota((8, LANES), 0)
+    lane2 = iota((8, LANES), 1)
+    for k in range(4):
+        tile_a = regrouped(partial[:4], k)
+        tile_b = regrouped([partial[4], extra, edge, faces], k)
+        for x in range(8):
+            send[pl.ds(k * 128 + x, 8, stride=16), :] = tile_a[x]
+            tile = tile_b[x]
+            if 1 <= x <= 5:
+                tile = jnp.where(lane2 // 32 == 1, eddies[x : x + 1, :], tile)
+            elif x == 6:
+                tile = jnp.where(lane2 // 32 == 1, 0.0, tile)
+            send[pl.ds(k * 128 + 8 + x, 8, stride=16), :] = tile
+
+
+def dot_nt(a, b, precision=None):
+    return lax.dot_general(
+        a, b, (((1,), (1,)), ((), ())), precision=precision, preferred_element_type=jnp.float32
+    )
+
+
+def span_hat(z, centre, span):
+    offset = z - centre + span / 2
+    offset = jnp.where(offset < 0, offset + span, jnp.where(offset >= span, offset - span, offset))
+    return HAT_PEAK * jnp.maximum(0.0, 1.0 - jnp.abs(offset - span / 2) / SIGMA_Z)
+
+
+def normal_hat(y, centre):
+    return HAT_PEAK * jnp.maximum(0.0, 1.0 - jnp.abs(y - centre) / SIGMA_Y)
+
+
+def ghost_flux(a, b, c):
+    mom = 1.0 + a
+    kinetic = mom * mom + b * b + c * c
+    q = [jnp.ones_like(mom), mom, b, c, 3.0 + 0.5 * kinetic]
+    return q
+
+
+def pencil_kernel(
+    received,
+    matrix,
+    partial,
+    velocity,
+    before,
+    after,
+    edge,
+    dilatation_bin,
+    vorticity_bin,
+    switch,
+    send,
+    updated_out,
+    energy_out,
+    weight_out,
+    ghost_planes,
+):
+    slab = lax.axis_index("gx")
+    core = lax.axis_index("gy")
+    slabs = lax.axis_size("gx")
+    first_core = core == 0
+    plane = (slab * 2 + core).astype(jnp.float32)
+    row = iota((8, LANES), 0)
+    lane = iota((8, LANES), 1)
+
+    tiles = [[received[g, h, 1] for g in range(16)] for h in range(2)]
+    chunks = []
+    for h in range(2):
+        for a in range(4):
+            out = None
+            for i in range(4):
+                moved = roll(tiles[h][4 * a + i], 32 * (i - 1), 1)
+                out = moved if out is None else jnp.where(lane // 32 == i, moved, out)
+            chunks.append(jnp.where((row >= 1) & (row <= 5), out, 0.0))
+    y_all = iota((64, LANES), 0).astype(jnp.float32)
+    left, right = [], []
+    for chunk in chunks:
+        left.append(chunk * span_hat(plane, chunk[2:3], 32.0))
+        right.append(normal_hat(y_all, chunk[1:2]))
+    inflow = dot_nt(
+        jnp.concatenate(left, axis=1), jnp.concatenate(right, axis=1), lax.Precision.HIGHEST
+    )
+    ghost = ghost_flux(inflow[3:4], inflow[4:5], inflow[5:6])
+    ghost_vel, ghost_pressure = velocity_pressure(ghost)
+    ghost_x = euler_flux(ghost, ghost_vel, ghost_pressure, 0)
+
+    @pl.when(slab == 0)
+    def _():
+        z_all = iota((32, LANES), 0).astype(jnp.float32)
+        y_own = (iota((32, LANES), 0) + core * 32).astype(jnp.float32)
+        lhs, rhs = [], []
+        for chunk in chunks:
+            hat = span_hat(z_all, chunk[2:3], 32.0)
+            lhs.append(jnp.concatenate([hat * chunk[3 + c : 4 + c] for c in range(3)], axis=0))
+            rhs.append(normal_hat(y_own, chunk[1:2]))
+        own = dot_nt(
+            jnp.concatenate(lhs, axis=1), jnp.concatenate(rhs, axis=1), lax.Precision.HIGHEST
+        )
+        parts = [
+            jnp.concatenate([own[c * 32 + 8 * k : c * 32 + 8 * k + 8] for k in range(4)], axis=1)
+            for c in range(3)
+        ]
+        q = ghost_flux(*parts)
+        for f in range(5):
+            ghost_planes[f] = q[f]
+
+    @pl.when(slab != 0)
+    def _():
+        ghost_planes[...] = before[...]
+
+    face_a, face_e = [], []
+    for h in range(2):
+        fa, fe = [], []
+        for g in range(16):
+            tile = tiles[h][g]
+            out = None
+            for f in range(4):
+                moved = roll(roll(tile, 32 * (f - 3), 1), -2 * f, 0)
+                out = moved if out is None else jnp.where(lane // 32 == f, moved, out)
+            fa.append(out)
+            fe.append(roll(tile, -32, 1))
+        face_a.append(fa)
+        face_e.append(fe)
+    columns_a, columns_e = [], []
+    for h in range(2):
+        ga = jnp.zeros((1, 32), jnp.float32)
+        own = slice(32 * h, 32 * h + 32)
+        ga = jnp.concatenate([ghost_x[f][:, own] for f in range(4)], axis=1)
+        ge = jnp.concatenate([ghost_x[4][:, own]] * 4, axis=1)
+        ca, ce = [], []
+        for g in range(16):
+            previous_a = face_a[h][g - 1] if g > 0 else ga
+            previous_e = face_e[h][g - 1] if g > 0 else ge
+            next_a = face_a[h][g + 1] if g < 15 else jnp.zeros((8, LANES), jnp.float32)
+            next_e = face_e[h][g + 1] if g < 15 else jnp.zeros((8, LANES), jnp.float32)
+            fix_a = jnp.where(row == 0, previous_a, jnp.where(row == 7, -next_a, 0.0))
+            fix_e = jnp.where(row == 0, previous_e, jnp.where(row == 7, -next_e, 0.0))
+            other = tiles[1 - h][g]
+            target = 31 if h == 0 else 0
+            side = -1.0 if h == 0 else 1.0
+            for f in range(4):
+                moved = roll(other, 32 * f + target - (64 + f), 1)
+                fix_a = jnp.where(lane == 32 * f + target, fix_a + side * moved, fix_a)
+            moved = roll(other, target - 68, 1)
+            fix_e = jnp.where(lane == target, fix_e + side * moved, fix_e)
+            ca.append(received[g, h, 0] + HALF_STEP * fix_a)
+            ce.append(jnp.where(lane < 32, tiles[h][g] + HALF_STEP * fix_e, 0.0))
+        columns_a.append(jnp.concatenate(ca, axis=0))
+        columns_e.append(jnp.concatenate(ce, axis=0))
+    columns = jnp.concatenate(
+        [columns_a[0], columns_a[1], columns_e[0] + roll(columns_e[1], 32, 1)], axis=1
+    )
+    smooth = lax.dot_general(
+        matrix[...],
+        columns,
+        (((1,), (0,)), ((), ())),
+        precision=lax.Precision.HIGHEST,
+        preferred_element_type=jnp.float32,
+    )
+
+    vel = [velocity[c] for c in range(3)]
+    planes = []
+    for ref, end in ((ghost_planes, 0), (after, 7)):
+        q = [ref[f][None] for f in range(5)]
+        halo_vel, halo_pressure = velocity_pressure(q)
+        planes.append((halo_vel, euler_flux(q, halo_vel, halo_pressure, 0)))
+    (before_vel, before_flux), (after_vel, after_flux) = planes
+    last_slab = slab == slabs - 1
+    lane3 = iota((8, 8, LANES), 2) % 32
+    halo = edge[...]
+
+    def y_halo(i):
+        near = jnp.where(first_core, roll(halo, 31 - i, 2), -roll(halo, -i, 2))
+        return jnp.where(lane3 == jnp.where(first_core, 31, 0), near, 0.0)
+
+    def x_all(c):
+        end = jnp.where(last_slab, vel[c][7:], after_vel[c])
+        return x_difference(vel[c], before_vel[c], end)
+
+    def y_all_(c):
+        return y_difference(vel[c], first_core) + y_halo(5 + c)
+
+    x_row = iota((8, 8, LANES), 0)
+    updated = []
+    for f in range(5):
+        flux_after = jnp.where(last_slab, 0.0, after_flux[f])
+        fix = jnp.where(x_row == 7, flux_after, jnp.where(x_row == 0, -before_flux[f], 0.0))
+        updated.append(partial[f] - HALF_STEP * (fix + y_halo(f)))
+    dx = [x_all(c) for c in range(3)]
+    dy = [y_all_(c) for c in range(3)]
+    dz = [z_difference(vel[c]) for c in range(3)]
+    dilatation = dx[0] + dy[1] + dz[2]
+    vort_x = dy[2] - dz[1]
+    vort_y = dz[0] - dx[2]
+    vort_z = dx[1] - dy[0]
+    squared = dilatation * dilatation
+    total = squared + vort_x * vort_x + vort_y * vort_y + vort_z * vort_z
+    sensor = squared / (total + 4.0 * SENSOR_EPS)
+    mask = jnp.concatenate([switch[...].astype(jnp.float32)] * 4, axis=1)
+    weight = sensor * mask[None]
+    for k in range(4):
+        updated_out[k] = regrouped(updated[:4], k)
+        energy_out[k] = roll(updated[4], -32 * k, 2)
+        weight_out[k] = regrouped([weight] * 4, k)
+
+    base = slab * 8 * HISTOGRAM_BINS // (8 * slabs)
+    dil = packed(dilatation_bin)
+    vort = (packed(vorticity_bin) - base) & (HISTOGRAM_BINS - 1)
+    levels = iota((HISTOGRAM_BINS, LANES), 0)
+    values, ones = [], []
+    for x in range(8):
+        for z in range(8):
+            values.append(jnp.where(vort[x, z : z + 1] == row, sensor[x, z : z + 1], 0.0))
+            ones.append(jnp.where(dil[x, z : z + 1] == levels, 1.0, 0.0).astype(jnp.bfloat16))
+    values = jnp.concatenate(values, axis=1)
+    high = values.astype(jnp.bfloat16)
+    low = (values - high.astype(jnp.float32)).astype(jnp.bfloat16)
+    ones = jnp.concatenate(ones, axis=1)
+    counts = dot_nt(jnp.concatenate([high, low], axis=0), ones)
+    counts = counts[:8] + counts[8:]
+    counts = jnp.concatenate([jnp.zeros((8, 64), jnp.float32), counts], axis=1)
+
+    for g in range(16):
+        block = smooth[8 * g : 8 * g + 8]
+        for h in range(2):
+            send[g, h, 0] = block[:, 128 * h : 128 * h + 128]
+            energy = roll(block[:, 256:], -32 * h, 1)
+            send[g, h, 1] = jnp.where(lane < 32, energy, counts)
+
+
+def final_kernel(scale, received, updated, energy, weight, conserved, histogram, totals):
+    for k in range(4):
+        for x in range(8):
+            w = weight[k, x]
+            smooth = received[pl.ds(k * 128 + x, 8, stride=16), :]
+            u = updated[k, x]
+            result = u + w * (smooth - u)
+            for f in range(4):
+                conserved[f, x, 8 * k : 8 * k + 8, :] = result[:, 32 * f : 32 * f + 32]
+            smooth = received[pl.ds(k * 128 + 8 + x, 8, stride=16), :]
+            u = energy[k, x]
+            result = u + w * (smooth - u)
+            conserved[4, x, 8 * k : 8 * k + 8, :] = result[:, :32]
+    totals[...] = jnp.zeros_like(totals)
+    for g in range(16):
+        both = received[32 * g + 8 : 32 * g + 16, :] + received[32 * g + 24 : 32 * g + 32, :]
+        totals[4 * g : 4 * g + 8, :] = totals[4 * g : 4 * g + 8, :] + both
+    first = totals[0:8, :] + totals[64:72, :]
+    table = jnp.concatenate([first, totals[8:64, :]], axis=0)[:, 64:]
+    histogram[...] = table.T * scale
+
+
+def shards(
+    density,
+    momentum,
+    energy,
+    eddy_normal_cell,
+    eddy_spanwise_cell,
+    eddy_signs,
+    eddy_strengths,
+    filter_matrices,
+    shock_switch,
+    dilatation_bin,
+    vorticity_bin,
+):
+    slabs, cores = lax.axis_size("gx"), lax.axis_size("gy")
+    shapes = (density.shape, eddy_strengths.shape, filter_matrices.shape, slabs, cores)
+    if shapes != ((8, 32, 32), (64,), (1, 128, 128), 16, 2):
+        return general_shards(
+            density,
+            momentum,
+            energy,
+            eddy_normal_cell,
+            eddy_spanwise_cell,
+            eddy_signs,
+            eddy_strengths,
+            filter_matrices,
+            shock_switch,
+            dilatation_bin,
+            vorticity_bin,
+        )
+    cells_x, span, cells_y = density.shape
+    total_y = cells_y * cores
+    total_eddies = eddy_strengths.shape[0] * slabs
+    amplitude = math.sqrt(total_y * span / (total_eddies * SIGMA_Y * SIGMA_Z))
+    plane = jax.ShapeDtypeStruct((5, 8, LANES), jnp.float32)
+    cells = (8, 8, LANES)
+    send, partial, velocity, first, last, edge = pl.pallas_call(
+        lambda *refs: slab_kernel(amplitude, *refs),
+        out_shape=[
+            jax.ShapeDtypeStruct((512, LANES), jnp.float32),
+            jax.ShapeDtypeStruct((5, *cells), jnp.float32),
+            jax.ShapeDtypeStruct((3, *cells), jnp.float32),
+            plane,
+            plane,
+            jax.ShapeDtypeStruct(cells, jnp.float32),
+        ],
+        name="slab",
+    )(
+        density,
+        momentum,
+        energy,
+        eddy_normal_cell.reshape(1, -1),
+        eddy_spanwise_cell.reshape(1, -1),
+        eddy_signs.T,
+        eddy_strengths.reshape(1, -1),
+    )
+    received = lax.all_to_all(send.reshape(32, 16, LANES), ("gx", "gy"), 0, 0, tiled=True)
+    up = [(i, i + 1) for i in range(slabs - 1)]
+    down = [(j, i) for i, j in up]
+    before = lax.ppermute(last, "gx", up)
+    after = lax.ppermute(first, "gx", down)
+    other_edge = lax.ppermute(edge, "gy", [(0, 1), (1, 0)])
+    send, updated, updated_energy, weight = pl.pallas_call(
+        pencil_kernel,
+        out_shape=[
+            jax.ShapeDtypeStruct((16, 2, 2, 8, LANES), jnp.float32),
+            jax.ShapeDtypeStruct((4, *cells), jnp.float32),
+            jax.ShapeDtypeStruct((4, *cells), jnp.float32),
+            jax.ShapeDtypeStruct((4, *cells), jnp.float32),
+        ],
+        scratch_shapes=[pltpu.VMEM((5, 8, LANES), jnp.float32)],
+        name="pencil",
+    )(
+        received.reshape(16, 2, 2, 8, LANES),
+        filter_matrices[0],
+        partial,
+        velocity,
+        before,
+        after,
+        other_edge,
+        dilatation_bin,
+        vorticity_bin,
+        shock_switch,
+    )
+    received = lax.all_to_all(send.reshape(32, 16, LANES), ("gx", "gy"), 0, 0, tiled=True)
+    scale = HISTOGRAM_BINS * HISTOGRAM_BINS / (cells_x * slabs * span * total_y)
+    conserved_next, histogram = pl.pallas_call(
+        lambda *refs: final_kernel(scale, *refs),
+        out_shape=[
+            jax.ShapeDtypeStruct((5, cells_x, span, cells_y), jnp.float32),
+            jax.ShapeDtypeStruct((HISTOGRAM_BINS, HISTOGRAM_BINS), jnp.float32),
+        ],
+        scratch_shapes=[pltpu.VMEM((72, LANES), jnp.float32)],
+        name="final",
+    )(received.reshape(512, LANES), updated, updated_energy, weight)
+    return (conserved_next, histogram)
+
+
 def solution(mesh):
     in_specs = (
         P("gx", None, "gy"),

time: 218 us -> 44 us (0.20)
  blocking collectives: 116 us -> 15.5 us
  local copies, waits for them, and re-layouts: 39.7 us -> 0.71 us
  other arithmetic: 21.8 us -> 0 us
  starting transfers between devices: 25 us -> 12.5 us
  Pallas kernels: 0 us -> 8.85 us
  matrix products: 5.55 us -> 0 us
    psum x2 -> x0, blocking collectives: 116 us -> none  [the longest x1 75.6 us: shards(): inflow = lax.psum(partial_sum, 'gx')]
    all_to_all x0 -> x1, blocking collectives: none -> 15.5 us  [shards(): lax.all_to_all(send.reshape(32, 16, LANES), ('gx', 'gy'), 0, 0, tiled=True)]
    unnamed x16 -> x14, local copies, waits for them, and re-layouts: 9.82 us -> 0.71 us
    pallas_call x0 -> x3, Pallas kernels: none -> 8.85 us  [the longest x1 3.99 us: shards(): pl.pallas_call(pencil_kernel, out_shape=[jax.ShapeDtypeStruct((16, 2, 2,...]
    scatter x4 -> x0, local copies, waits for them, and re-layouts: 7.3 us -> none  [the longest x1 3.73 us: shards(): padded.at[:, 1:-1, :, -1]]
    all_to_all x3 -> x1, starting transfers between devices: 13.9 us -> 7.3 us  [shards(): lax.all_to_all(send.reshape(32, 16, LANES), ('gx', 'gy'), 0, 0, tiled=True)]
    dynamic_slice x16 -> x0, local copies, waits for them, and re-layouts: 6 us -> none  [plane_histogram(): lax.scan(accumulate_plane, jnp.zeros((HISTOGRAM_BINS, HISTOGRAM_BINS), jn...]
    ppermute x4 -> x3, starting transfers between devices: 11.1 us -> 5.18 us  [the longest x1 3.57 us: shards(): before = lax.ppermute(last, 'gx', up)]
  transfers between devices with their start and end apart: 7 -> 4, of which waited for: 1 -> 3; matrix products, arithmetic and copies ran while one was open for 14% -> 0% of each run, Pallas kernels for 0% -> 0%
where the time goes in v1:
time: 44 us; the launch traced here: 43.6 us
  blocking collectives  15.5 us (35%)
  starting transfers between devices  12.5 us (28%)
  Pallas kernels  8.85 us (20%)
  waiting for transfers between devices  5.37 us (12%)
  local copies, waits for them, and re-layouts  0.71 us (2%)
  between operations  0.7 us (2%)
    all_to_all x1, blocking collectives, shards(): lax.all_to_all(send.reshape(32, 16, LANES), ('gx', 'gy'), 0, 0, tiled=True)  15.5 us
    all_to_all x1, starting transfers between devices, shards(): lax.all_to_all(send.reshape(32, 16, LANES), ('gx', 'gy'), 0, 0, tiled=True)  7.3 us
    ppermute x1, waiting for transfers between devices, shards(): after = lax.ppermute(first, 'gx', down)  4.22 us
    pallas_call x1, Pallas kernels, shards(): pl.pallas_call(pencil_kernel, out_shape=[jax.ShapeDtypeStruct((16, 2, 2,...  3.99 us
    ppermute x1, starting transfers between devices, shards(): before = lax.ppermute(last, 'gx', up)  3.57 us
    pallas_call x1, Pallas kernels, shards(): pl.pallas_call(lambda *refs: slab_kernel(amplitude, *refs), out_shape=[ja...  2.64 us
    pallas_call x1, Pallas kernels, shards(): pl.pallas_call(lambda *refs: final_kernel(scale, *refs), out_shape=[jax.S...  2.22 us
    ppermute x1, starting transfers between devices, shards(): after = lax.ppermute(first, 'gx', down)  1.29 us
  transfers between devices with their start and end apart: 4, of which 3 were waited for; matrix products, arithmetic and copies ran while one was open for 0% of the time, Pallas kernels for 0%

profile of v1, /device:TPU:0, one launch (start us, length us, event | category | flops | bytes accessed | tf_op | source)
XLA Modules:
  0.0 43.6 jit_solution(7977322318952867290)
XLA Ops:
  0.6 2.6 %slab.1 = (f32[512,128]{1,0:T(8,128)}, f32[5,8,8,128]{3,2,1,0:T(8,128)}, f32[3,8,8,128]{3,2,1,0:T(8,128)}, f32[5,8,128]{2,1,0:T(8,128)}, f32[5,8,128]{2,1,0:T(8,128)}, /*index=5*/f32[8,8,128]{2,1,0:T(8,128)}) custom-call(f32[8,32,32]{2,1,0:T(8,128)} %refs_0_.1, f32[3,8,32,32]{3,2,1,0:T(8,128)} %refs_1_.1, f32[8,32,32]{2,1,0:T(8,128)} %refs_2_.1, ...), custom_call_target="tpu_custom_call" | custom-call | tf_op jit(solution)/shard_map/slab/pallas_call | solution.py:608
  3.3 0.0 copy-start.4
  3.3 0.0 copy-start.6
  3.3 0.0 copy-start.5
  3.3 7.3 %all-to-all-start = ((f32[32,16,128]{2,1,0:T(8,128)}), f32[32,16,128]{2,1,0:T(8,128)S(1)}, u32[]{:S(2)}, u32[]{:S(2)}) async-start(f32[32,16,128]{2,1,0:T(8,128)} %bitcast.11), calls=%async_computation | async-start | bytes 524288 | tf_op jit(solution)/shard_map/all_to_all | solution.py:628
  10.6 0.0 copy-done.4
  10.6 0.3 collective-permute-start.2
  10.9 0.0 copy-done.6
  10.9 3.6 %collective-permute-start = (f32[5,8,128]{2,1,0:T(8,128)S(1)}, f32[5,8,128]{2,1,0:T(8,128)S(1)}, u32[]{:S(2)}, u32[]{:S(2)}) collective-permute-start(f32[5,8,128]{2,1,0:T(8,128)S(1)} %copy-done.6), channel_id=1, source_target_pairs={{0,2},{2,4},{4,6},{6,8},{8,10},{10,12},{12,14},{14,16},{16,18},{18... | collective-permute-start | bytes 61448 | tf_op jit(solution)/shard_map/ppermute | solution.py:631
  14.5 0.0 copy-done.5
  14.5 1.3 %collective-permute-start.1 = (f32[5,8,128]{2,1,0:T(8,128)S(1)}, f32[5,8,128]{2,1,0:T(8,128)S(1)}, u32[]{:S(2)}, u32[]{:S(2)}) collective-permute-start(f32[5,8,128]{2,1,0:T(8,128)S(1)} %copy-done.5), channel_id=1, source_target_pairs={{2,0},{4,2},{6,4},{8,6},{10,8},{12,10},{14,12},{16,14},{18,16},{20... | collective-permute-start | bytes 61448 | tf_op jit(solution)/shard_map/ppermute | solution.py:632
  15.8 0.2 collective-permute-done.before
  16.0 0.0 copy-start.2
  16.0 4.2 %collective-permute-done.1.after = f32[5,8,128]{2,1,0:T(8,128)S(1)} collective-permute-done((f32[5,8,128]{2,1,0:T(8,128)S(1)}, f32[5,8,128]{2,1,0:T(8,128)S(1)}, u32[]{:S(2)}, u32[]{:S(2)}) %collective-permute-start.1) | collective-permute-done | bytes 20512 | tf_op jit(solution)/shard_map/ppermute | solution.py:632
  20.2 0.0 copy-start.3
  20.2 0.0 collective-permute-done.2.edge
  20.2 1.0 %all-to-all-done = f32[32,16,128]{2,1,0:T(8,128)S(1)} async-done(((f32[32,16,128]{2,1,0:T(8,128)}), f32[32,16,128]{2,1,0:T(8,128)S(1)}, u32[]{:S(2)}, u32[]{:S(2)}) %all-to-all-start) | async-done | bytes 262176 | tf_op jit(solution)/shard_map/all_to_all | solution.py:628
  21.2 0.0 copy-done.2
  21.2 0.0 copy-done.3
  21.2 0.0 copy-done.1
  21.2 0.7 %copy-done = f32[32,16,128]{2,1,0:T(8,128)} copy-done((f32[32,16,128]{2,1,0:T(8,128)}, f32[32,16,128]{2,1,0:T(8,128)S(1)}, u32[]{:S(2)}) %copy-start) | copy-done | bytes 262168
  21.9 4.0 %pencil.1 = (f32[16,2,2,8,128]{4,3,2,1,0:T(8,128)}, f32[4,8,8,128]{3,2,1,0:T(8,128)}, f32[4,8,8,128]{3,2,1,0:T(8,128)}, f32[4,8,8,128]{3,2,1,0:T(8,128)}) custom-call(f32[16,2,2,8,128]{4,3,2,1,0:T(8,128)} %bitcast.9, f32[128,128]{1,0:T(8,128)} %bitcast.13, f32[5,8,8,128]{3,2,1,0:T(8,128)} %get-tuple-element.13.partial, ...), custom_call_target="tpu_custom_call" | custom-call | tf_op jit(solution)/shard_map/pencil/pallas_call | solution.py:634
  25.9 15.5 %all_to_all.10 = f32[32,16,128]{2,1,0:T(8,128)} all-to-all(f32[32,16,128]{2,1,0:T(8,128)} %bitcast.12), channel_id=1, replica_groups=mesh['gx'=16,'gy'=2] {'gx','gy'}, dimensions={0} | all-to-all | bytes 524288 | tf_op jit(solution)/shard_map/all_to_all | solution.py:656
  41.4 2.2 %final.1 = (f32[5,8,32,32]{3,2,1,0:T(8,128)}, f32[64,64]{1,0:T(8,128)}) custom-call(f32[512,128]{1,0:T(8,128)} %bitcast.10, f32[4,8,8,128]{3,2,1,0:T(8,128)} %get-tuple-element.19.refs_1_, f32[4,8,8,128]{3,2,1,0:T(8,128)} %get-tuple-element.20.refs_2_, f32[4,8,8,128]{3,2,1,0:T(8,128)} %get-tuple-element.21.refs_3_), custom_call_target="tpu_custom_call" | custom-call | tf_op jit(solution)/shard_map/final/pallas_call | solution.py:658
  (2 shorter events, 0.0 us)
Async XLA Ops:
  3.3 7.3 %copy-start.4 = (f32[8,8,128]{2,1,0:T(8,128)S(1)}, f32[8,8,128]{2,1,0:T(8,128)}, u32[]{:S(2)}) copy-start(f32[8,8,128]{2,1,0:T(8,128)} %get-tuple-element.17) | copy-start | bytes 98308
  3.3 7.7 %copy-start.6 = (f32[5,8,128]{2,1,0:T(8,128)S(1)}, f32[5,8,128]{2,1,0:T(8,128)}, u32[]{:S(2)}) copy-start(f32[5,8,128]{2,1,0:T(8,128)} %get-tuple-element.15) | copy-start | bytes 61444
  3.3 11.2 %copy-start.5 = (f32[5,8,128]{2,1,0:T(8,128)S(1)}, f32[5,8,128]{2,1,0:T(8,128)}, u32[]{:S(2)}) copy-start(f32[5,8,128]{2,1,0:T(8,128)} %get-tuple-element.16) | copy-start | bytes 61444
  3.3 17.9 %all-to-all-start = ((f32[32,16,128]{2,1,0:T(8,128)}), f32[32,16,128]{2,1,0:T(8,128)S(1)}, u32[]{:S(2)}, u32[]{:S(2)}) async-start(f32[32,16,128]{2,1,0:T(8,128)} %bitcast.11), calls=%async_computation | async-start | bytes 524288 | tf_op jit(solution)/shard_map/all_to_all | solution.py:628
  10.6 9.6 %collective-permute-start.2 = (f32[8,8,128]{2,1,0:T(8,128)S(1)}, f32[8,8,128]{2,1,0:T(8,128)S(1)}, u32[]{:S(2)}, u32[]{:S(2)}) collective-permute-start(f32[8,8,128]{2,1,0:T(8,128)S(1)} %copy-done.4), channel_id=1, source_target_pairs={{0,1},{1,0},{2,3},{3,2},{4,5},{5,4},{6,7},{7,6},{8,9},{9,8},{10,11... | collective-permute-start | bytes 98312 | tf_op jit(solution)/shard_map/ppermute | solution.py:633
  10.9 5.0 %collective-permute-start = (f32[5,8,128]{2,1,0:T(8,128)S(1)}, f32[5,8,128]{2,1,0:T(8,128)S(1)}, u32[]{:S(2)}, u32[]{:S(2)}) collective-permute-start(f32[5,8,128]{2,1,0:T(8,128)S(1)} %copy-done.6), channel_id=1, source_target_pairs={{0,2},{2,4},{4,6},{6,8},{8,10},{10,12},{12,14},{14,16},{16,18},{18... | collective-permute-start | bytes 61448 | tf_op jit(solution)/shard_map/ppermute | solution.py:631
  14.5 5.7 %collective-permute-start.1 = (f32[5,8,128]{2,1,0:T(8,128)S(1)}, f32[5,8,128]{2,1,0:T(8,128)S(1)}, u32[]{:S(2)}, u32[]{:S(2)}) collective-permute-start(f32[5,8,128]{2,1,0:T(8,128)S(1)} %copy-done.5), channel_id=1, source_target_pairs={{2,0},{4,2},{6,4},{8,6},{10,8},{12,10},{14,12},{16,14},{18,16},{20... | collective-permute-start | bytes 61448 | tf_op jit(solution)/shard_map/ppermute | solution.py:632
  16.0 5.2 %copy-start.2 = (f32[5,8,128]{2,1,0:T(8,128)}, f32[5,8,128]{2,1,0:T(8,128)S(1)}, u32[]{:S(2)}) copy-start(f32[5,8,128]{2,1,0:T(8,128)S(1)} %collective-permute-done.before) | copy-start | bytes 61444
  20.2 1.0 %copy-start.3 = (f32[5,8,128]{2,1,0:T(8,128)}, f32[5,8,128]{2,1,0:T(8,128)S(1)}, u32[]{:S(2)}) copy-start(f32[5,8,128]{2,1,0:T(8,128)S(1)} %collective-permute-done.1.after) | copy-start | bytes 61444
  20.2 1.0 %copy-start.1 = (f32[8,8,128]{2,1,0:T(8,128)}, f32[8,8,128]{2,1,0:T(8,128)S(1)}, u32[]{:S(2)}) copy-start(f32[8,8,128]{2,1,0:T(8,128)S(1)} %collective-permute-done.2.edge) | copy-start | bytes 98308
  21.2 0.7 %copy-start = (f32[32,16,128]{2,1,0:T(8,128)}, f32[32,16,128]{2,1,0:T(8,128)S(1)}, u32[]{:S(2)}) copy-start(f32[32,16,128]{2,1,0:T(8,128)S(1)} %all-to-all-done) | copy-start | bytes 786436

commit v2 on v1

--- a/solution.py
+++ b/solution.py
@@ -209,7 +209,8 @@
 
 
 def packed(ref, *lead):
-    parts = [ref[(*lead, slice(None), pl.ds(8 * k, 8), slice(None))] for k in range(4)]
+    lead = lead if len(lead) == len(ref.shape) - 2 else (*lead, slice(None))
+    parts = [ref[(*lead, pl.ds(8 * k, 8), slice(None))] for k in range(4)]
     return jnp.concatenate(parts, axis=-1)
 
 
@@ -267,8 +268,6 @@
     signs,
     strengths,
     send,
-    partial_out,
-    velocity_out,
     first_out,
     last_out,
     edge_out,
@@ -289,11 +288,8 @@
         change = change + y_difference(flux_y[f], first_core)
         change = change + z_difference(flux_z[f])
         partial.append(q[f] - HALF_STEP * change)
-        partial_out[f] = partial[f]
         first_out[f] = q[f][0]
         last_out[f] = q[f][7]
-    for c in range(3):
-        velocity_out[c] = vel[c]
 
     lane = iota((8, 8, LANES), 2) % 32
     edge = jnp.zeros((8, 8, LANES), jnp.float32)
@@ -335,40 +331,126 @@
             send[pl.ds(k * 128 + 8 + x, 8, stride=16), :] = tile
 
 
-def dot_nt(a, b, precision=None):
+def dot_nt(a, b):
     return lax.dot_general(
-        a, b, (((1,), (1,)), ((), ())), precision=precision, preferred_element_type=jnp.float32
-    )
+        a, b, (((1,), (1,)), ((), ())), preferred_element_type=jnp.float32
+    )
+
+
+def halves(a):
+    high = a.astype(jnp.bfloat16)
+    return high, (a - high.astype(jnp.float32)).astype(jnp.bfloat16)
 
 
 def span_hat(z, centre, span):
     offset = z - centre + span / 2
     offset = jnp.where(offset < 0, offset + span, jnp.where(offset >= span, offset - span, offset))
-    return HAT_PEAK * jnp.maximum(0.0, 1.0 - jnp.abs(offset - span / 2) / SIGMA_Z)
+    return jnp.maximum(0.0, 1.0 - jnp.abs(offset - span / 2) * (1.0 / SIGMA_Z))
 
 
 def normal_hat(y, centre):
-    return HAT_PEAK * jnp.maximum(0.0, 1.0 - jnp.abs(y - centre) / SIGMA_Y)
-
-
-def ghost_flux(a, b, c):
+    return jnp.maximum(0.0, 1.0 - jnp.abs(y - centre) * (1.0 / SIGMA_Y)).astype(jnp.bfloat16)
+
+
+def ghost_state_rows(a, b, c):
     mom = 1.0 + a
     kinetic = mom * mom + b * b + c * c
-    q = [jnp.ones_like(mom), mom, b, c, 3.0 + 0.5 * kinetic]
-    return q
-
-
-def pencil_kernel(
-    received,
-    matrix,
-    partial,
-    velocity,
-    before,
-    after,
+    return [jnp.ones_like(mom), mom, b, c, 3.0 + 0.5 * kinetic]
+
+
+def sensor_of(d, vort_x, vort_y, vort_z):
+    squared = d * d
+    total = squared + vort_x * vort_x + vort_y * vort_y + vort_z * vort_z
+    return squared / (total + 4.0 * SENSOR_EPS)
+
+
+def counted(sensor, dil, vort):
+    row = iota((8, LANES), 0)
+    levels = iota((HISTOGRAM_BINS, LANES), 0)
+    values, ones = [], []
+    for x in range(len(sensor)):
+        for z in range(8):
+            values.append(jnp.where(vort[x][z : z + 1] == row, sensor[x][z : z + 1], 0.0))
+            ones.append(jnp.where(dil[x][z : z + 1] == levels, 1.0, 0.0).astype(jnp.bfloat16))
+    high, low = halves(jnp.concatenate(values, axis=1))
+    counts = dot_nt(jnp.concatenate([high, low], axis=0), jnp.concatenate(ones, axis=1))
+    return counts[:8] + counts[8:]
+
+
+def slab_bins(vorticity_bin, rows):
+    slab = lax.axis_index("gx")
+    base = slab * HISTOGRAM_BINS // lax.axis_size("gx")
+    return (packed(vorticity_bin, rows) - base) & (HISTOGRAM_BINS - 1)
+
+
+def interior_kernel(
+    density,
+    momentum,
+    energy,
     edge,
     dilatation_bin,
     vorticity_bin,
     switch,
+    updated_out,
+    energy_out,
+    weight_out,
+    ends_out,
+    counts_out,
+):
+    first_core = lax.axis_index("gy") == 0
+    last_slab = lax.axis_index("gx") == lax.axis_size("gx") - 1
+    q = [packed(density)] + [packed(momentum, c) for c in range(3)] + [packed(energy)]
+    vel, pressure = velocity_pressure(q)
+    flux_x = euler_flux(q, vel, pressure, 0)
+    flux_y = euler_flux(q, vel, pressure, 1)
+    flux_z = euler_flux(q, vel, pressure, 2)
+    zero = jnp.zeros((1, 8, LANES), jnp.float32)
+    lane = iota((8, 8, LANES), 2) % 32
+    halo = edge[...]
+
+    def y_whole(a, i):
+        near = jnp.where(first_core, roll(halo, 31 - i, 2), -roll(halo, -i, 2))
+        near = jnp.where(lane == jnp.where(first_core, 31, 0), near, 0.0)
+        return y_difference(a, first_core) + near
+
+    updated = []
+    for f in range(5):
+        after = jnp.where(last_slab, flux_x[f][7:], 0.0)
+        change = x_difference(flux_x[f], zero, after)
+        change = change + y_whole(flux_y[f], f) + z_difference(flux_z[f])
+        updated.append(q[f] - HALF_STEP * change)
+    dx = [x_difference(a, zero, jnp.where(last_slab, a[7:], 0.0)) for a in vel]
+    dy = [y_whole(vel[c], 5 + c) for c in range(3)]
+    dz = [z_difference(a) for a in vel]
+    rates = [dx[0] + dy[1] + dz[2], dy[2] - dz[1], dz[0] - dx[2], dx[1] - dy[0]]
+    sensor = sensor_of(*rates)
+    mask = jnp.concatenate([switch[...].astype(jnp.float32)] * 4, axis=1)
+    weight = sensor * mask[None]
+    for k in range(4):
+        updated_out[k] = regrouped(updated[:4], k)
+        energy_out[k] = roll(updated[4], -32 * k, 2)
+        weight_out[k] = regrouped([weight] * 4, k)
+    for i, a in enumerate(updated + rates):
+        ends_out[i, 0] = a[0]
+        ends_out[i, 1] = a[7]
+    dil = packed(dilatation_bin)
+    vort = slab_bins(vorticity_bin, slice(None))
+    inner = range(1, 7)
+    counts_out[...] = counted(
+        [sensor[x] for x in inner], [dil[x] for x in inner], [vort[x] for x in inner]
+    )
+
+
+def pencil_kernel(
+    received,
+    matrix,
+    ends,
+    before,
+    after,
+    dilatation_bin,
+    vorticity_bin,
+    switch,
+    counts_in,
     send,
     updated_out,
     energy_out,
@@ -377,11 +459,11 @@
 ):
     slab = lax.axis_index("gx")
     core = lax.axis_index("gy")
-    slabs = lax.axis_size("gx")
-    first_core = core == 0
+    last_slab = slab == lax.axis_size("gx") - 1
     plane = (slab * 2 + core).astype(jnp.float32)
     row = iota((8, LANES), 0)
     lane = iota((8, LANES), 1)
+    peak = HAT_PEAK * HAT_PEAK
 
     tiles = [[received[g, h, 1] for g in range(16)] for h in range(2)]
     chunks = []
@@ -391,16 +473,17 @@
             for i in range(4):
                 moved = roll(tiles[h][4 * a + i], 32 * (i - 1), 1)
                 out = moved if out is None else jnp.where(lane // 32 == i, moved, out)
-            chunks.append(jnp.where((row >= 1) & (row <= 5), out, 0.0))
+            chunks.append(out)
     y_all = iota((64, LANES), 0).astype(jnp.float32)
-    left, right = [], []
+    lhs, rhs = [], []
     for chunk in chunks:
-        left.append(chunk * span_hat(plane, chunk[2:3], 32.0))
-        right.append(normal_hat(y_all, chunk[1:2]))
-    inflow = dot_nt(
-        jnp.concatenate(left, axis=1), jnp.concatenate(right, axis=1), lax.Precision.HIGHEST
-    )
-    ghost = ghost_flux(inflow[3:4], inflow[4:5], inflow[5:6])
+        weighted = (chunk * peak) * span_hat(plane, chunk[2:3], 32.0)
+        lhs.append(jnp.where((row >= 3) & (row <= 5), weighted, 0.0))
+        rhs.append(normal_hat(y_all, chunk[1:2]))
+    high, low = halves(jnp.concatenate(lhs, axis=1))
+    inflow = dot_nt(jnp.concatenate([high, low], axis=0), jnp.concatenate(rhs, axis=1))
+    inflow = inflow[:8] + inflow[8:]
+    ghost = ghost_state_rows(inflow[3:4], inflow[4:5], inflow[5:6])
     ghost_vel, ghost_pressure = velocity_pressure(ghost)
     ghost_x = euler_flux(ghost, ghost_vel, ghost_pressure, 0)
 
@@ -410,17 +493,17 @@
         y_own = (iota((32, LANES), 0) + core * 32).astype(jnp.float32)
         lhs, rhs = [], []
         for chunk in chunks:
-            hat = span_hat(z_all, chunk[2:3], 32.0)
+            hat = span_hat(z_all, chunk[2:3], 32.0) * peak
             lhs.append(jnp.concatenate([hat * chunk[3 + c : 4 + c] for c in range(3)], axis=0))
             rhs.append(normal_hat(y_own, chunk[1:2]))
-        own = dot_nt(
-            jnp.concatenate(lhs, axis=1), jnp.concatenate(rhs, axis=1), lax.Precision.HIGHEST
-        )
+        high, low = halves(jnp.concatenate(lhs, axis=1))
+        own = dot_nt(jnp.concatenate([high, low], axis=0), jnp.concatenate(rhs, axis=1))
+        own = own[:96] + own[96:]
         parts = [
             jnp.concatenate([own[c * 32 + 8 * k : c * 32 + 8 * k + 8] for k in range(4)], axis=1)
             for c in range(3)
         ]
-        q = ghost_flux(*parts)
+        q = ghost_state_rows(*parts)
         for f in range(5):
             ghost_planes[f] = q[f]
 
@@ -443,16 +526,14 @@
         face_e.append(fe)
     columns_a, columns_e = [], []
     for h in range(2):
-        ga = jnp.zeros((1, 32), jnp.float32)
         own = slice(32 * h, 32 * h + 32)
-        ga = jnp.concatenate([ghost_x[f][:, own] for f in range(4)], axis=1)
-        ge = jnp.concatenate([ghost_x[4][:, own]] * 4, axis=1)
+        ghost_a = jnp.concatenate([ghost_x[f][:, own] for f in range(4)], axis=1)
+        ghost_e = jnp.concatenate([ghost_x[4][:, own]] * 4, axis=1)
         ca, ce = [], []
         for g in range(16):
-            previous_a = face_a[h][g - 1] if g > 0 else ga
-            previous_e = face_e[h][g - 1] if g > 0 else ge
-            next_a = face_a[h][g + 1] if g < 15 else jnp.zeros((8, LANES), jnp.float32)
-            next_e = face_e[h][g + 1] if g < 15 else jnp.zeros((8, LANES), jnp.float32)
+            zero = jnp.zeros((8, LANES), jnp.float32)
+            previous_a, previous_e = (face_a[h][g - 1], face_e[h][g - 1]) if g else (ghost_a, ghost_e)
+            next_a, next_e = (face_a[h][g + 1], face_e[h][g + 1]) if g < 15 else (zero, zero)
             fix_a = jnp.where(row == 0, previous_a, jnp.where(row == 7, -next_a, 0.0))
             fix_e = jnp.where(row == 0, previous_e, jnp.where(row == 7, -next_e, 0.0))
             other = tiles[1 - h][g]
@@ -470,96 +551,74 @@
     columns = jnp.concatenate(
         [columns_a[0], columns_a[1], columns_e[0] + roll(columns_e[1], 32, 1)], axis=1
     )
-    smooth = lax.dot_general(
-        matrix[...],
-        columns,
-        (((1,), (0,)), ((), ())),
-        precision=lax.Precision.HIGHEST,
-        preferred_element_type=jnp.float32,
-    )
-
-    vel = [velocity[c] for c in range(3)]
-    planes = []
-    for ref, end in ((ghost_planes, 0), (after, 7)):
-        q = [ref[f][None] for f in range(5)]
-        halo_vel, halo_pressure = velocity_pressure(q)
-        planes.append((halo_vel, euler_flux(q, halo_vel, halo_pressure, 0)))
-    (before_vel, before_flux), (after_vel, after_flux) = planes
-    last_slab = slab == slabs - 1
-    lane3 = iota((8, 8, LANES), 2) % 32
-    halo = edge[...]
-
-    def y_halo(i):
-        near = jnp.where(first_core, roll(halo, 31 - i, 2), -roll(halo, -i, 2))
-        return jnp.where(lane3 == jnp.where(first_core, 31, 0), near, 0.0)
-
-    def x_all(c):
-        end = jnp.where(last_slab, vel[c][7:], after_vel[c])
-        return x_difference(vel[c], before_vel[c], end)
-
-    def y_all_(c):
-        return y_difference(vel[c], first_core) + y_halo(5 + c)
-
-    x_row = iota((8, 8, LANES), 0)
-    updated = []
-    for f in range(5):
-        flux_after = jnp.where(last_slab, 0.0, after_flux[f])
-        fix = jnp.where(x_row == 7, flux_after, jnp.where(x_row == 0, -before_flux[f], 0.0))
-        updated.append(partial[f] - HALF_STEP * (fix + y_halo(f)))
-    dx = [x_all(c) for c in range(3)]
-    dy = [y_all_(c) for c in range(3)]
-    dz = [z_difference(vel[c]) for c in range(3)]
-    dilatation = dx[0] + dy[1] + dz[2]
-    vort_x = dy[2] - dz[1]
-    vort_y = dz[0] - dx[2]
-    vort_z = dx[1] - dy[0]
-    squared = dilatation * dilatation
-    total = squared + vort_x * vort_x + vort_y * vort_y + vort_z * vort_z
-    sensor = squared / (total + 4.0 * SENSOR_EPS)
+    m_high, m_low = halves(matrix[...])
+    c_high, c_low = halves(columns)
+    smooth = (
+        jnp.dot(m_high, c_high, preferred_element_type=jnp.float32)
+        + jnp.dot(m_high, c_low, preferred_element_type=jnp.float32)
+        + jnp.dot(m_low, c_high, preferred_element_type=jnp.float32)
+    )
+
+    sensors, dils, vorts = [], [], []
     mask = jnp.concatenate([switch[...].astype(jnp.float32)] * 4, axis=1)
-    weight = sensor * mask[None]
-    for k in range(4):
-        updated_out[k] = regrouped(updated[:4], k)
-        energy_out[k] = roll(updated[4], -32 * k, 2)
-        weight_out[k] = regrouped([weight] * 4, k)
-
-    base = slab * 8 * HISTOGRAM_BINS // (8 * slabs)
-    dil = packed(dilatation_bin)
-    vort = (packed(vorticity_bin) - base) & (HISTOGRAM_BINS - 1)
-    levels = iota((HISTOGRAM_BINS, LANES), 0)
-    values, ones = [], []
-    for x in range(8):
-        for z in range(8):
-            values.append(jnp.where(vort[x, z : z + 1] == row, sensor[x, z : z + 1], 0.0))
-            ones.append(jnp.where(dil[x, z : z + 1] == levels, 1.0, 0.0).astype(jnp.bfloat16))
-    values = jnp.concatenate(values, axis=1)
-    high = values.astype(jnp.bfloat16)
-    low = (values - high.astype(jnp.float32)).astype(jnp.bfloat16)
-    ones = jnp.concatenate(ones, axis=1)
-    counts = dot_nt(jnp.concatenate([high, low], axis=0), ones)
-    counts = counts[:8] + counts[8:]
+    for end, ref in ((0, ghost_planes), (1, after)):
+        q = [ref[f] for f in range(5)]
+        vel, pressure = velocity_pressure(q)
+        flux = euler_flux(q, vel, pressure, 0)
+        sign = -1.0 if end == 0 else 1.0
+        add = [sign * a for a in flux + vel]
+        if end == 1:
+            add = [jnp.where(last_slab, 0.0, a) for a in add]
+        updated = [ends[f, end] - HALF_STEP * add[f] for f in range(5)]
+        rates = [ends[5 + i, end] for i in range(4)]
+        rates = [rates[0] + add[5], rates[1], rates[2] - add[7], rates[3] + add[6]]
+        sensor = sensor_of(*rates)
+        weight = sensor * mask
+        for k in range(4):
+            updated_out[end, k] = regrouped(updated[:4], k)
+            energy_out[end, k] = roll(updated[4], -32 * k, 1)
+            weight_out[end, k] = regrouped([weight] * 4, k)
+        at = pl.ds(7 * end, 1)
+        sensors.append(sensor)
+        dils.append(packed(dilatation_bin, at)[0])
+        vorts.append(slab_bins(vorticity_bin, at)[0])
+    counts = counts_in[...] + counted(sensors, dils, vorts)
     counts = jnp.concatenate([jnp.zeros((8, 64), jnp.float32), counts], axis=1)
 
     for g in range(16):
         block = smooth[8 * g : 8 * g + 8]
         for h in range(2):
             send[g, h, 0] = block[:, 128 * h : 128 * h + 128]
-            energy = roll(block[:, 256:], -32 * h, 1)
-            send[g, h, 1] = jnp.where(lane < 32, energy, counts)
-
-
-def final_kernel(scale, received, updated, energy, weight, conserved, histogram, totals):
+            own_energy = roll(block[:, 256:], -32 * h, 1)
+            send[g, h, 1] = jnp.where(lane < 32, own_energy, counts)
+
+
+def final_kernel(
+    scale,
+    received,
+    updated,
+    energy,
+    weight,
+    end_updated,
+    end_energy,
+    end_weight,
+    conserved,
+    histogram,
+    totals,
+):
     for k in range(4):
         for x in range(8):
-            w = weight[k, x]
+            if x in (0, 7):
+                end = x // 7
+                u, e, w = end_updated[end, k], end_energy[end, k], end_weight[end, k]
+            else:
+                u, e, w = updated[k, x], energy[k, x], weight[k, x]
             smooth = received[pl.ds(k * 128 + x, 8, stride=16), :]
-            u = updated[k, x]
             result = u + w * (smooth - u)
             for f in range(4):
                 conserved[f, x, 8 * k : 8 * k + 8, :] = result[:, 32 * f : 32 * f + 32]
             smooth = received[pl.ds(k * 128 + 8 + x, 8, stride=16), :]
-            u = energy[k, x]
-            result = u + w * (smooth - u)
+            result = e + w * (smooth - e)
             conserved[4, x, 8 * k : 8 * k + 8, :] = result[:, :32]
     totals[...] = jnp.zeros_like(totals)
     for g in range(16):
@@ -605,16 +664,12 @@
     amplitude = math.sqrt(total_y * span / (total_eddies * SIGMA_Y * SIGMA_Z))
     plane = jax.ShapeDtypeStruct((5, 8, LANES), jnp.float32)
     cells = (8, 8, LANES)
-    send, partial, velocity, first, last, edge = pl.pallas_call(
+    f32 = lambda *shape: jax.ShapeDtypeStruct(shape, jnp.float32)
+    vmem = lambda *shape: pltpu.VMEM(shape, jnp.float32)
+    near = lambda a: pltpu.with_memory_space_constraint(a, pltpu.VMEM)
+    send, first, last, edge = pl.pallas_call(
         lambda *refs: slab_kernel(amplitude, *refs),
-        out_shape=[
-            jax.ShapeDtypeStruct((512, LANES), jnp.float32),
-            jax.ShapeDtypeStruct((5, *cells), jnp.float32),
-            jax.ShapeDtypeStruct((3, *cells), jnp.float32),
-            plane,
-            plane,
-            jax.ShapeDtypeStruct(cells, jnp.float32),
-        ],
+        out_shape=[vmem(512, LANES), vmem(5, 8, LANES), vmem(5, 8, LANES), vmem(*cells)],
         name="slab",
     )(
         density,
@@ -631,39 +686,36 @@
     before = lax.ppermute(last, "gx", up)
     after = lax.ppermute(first, "gx", down)
     other_edge = lax.ppermute(edge, "gy", [(0, 1), (1, 0)])
-    send, updated, updated_energy, weight = pl.pallas_call(
+    updated, updated_energy, weight, ends, counts = pl.pallas_call(
+        interior_kernel,
+        out_shape=[vmem(4, *cells), vmem(4, *cells), vmem(4, *cells), vmem(9, 2, 8, LANES), vmem(8, 64)],
+        cost_estimate=pl.CostEstimate(flops=10_000_000, bytes_accessed=2_000_000, transcendentals=0),
+        name="interior",
+    )(density, momentum, energy, near(other_edge), dilatation_bin, vorticity_bin, shock_switch)
+    send, *end_rows = pl.pallas_call(
         pencil_kernel,
-        out_shape=[
-            jax.ShapeDtypeStruct((16, 2, 2, 8, LANES), jnp.float32),
-            jax.ShapeDtypeStruct((4, *cells), jnp.float32),
-            jax.ShapeDtypeStruct((4, *cells), jnp.float32),
-            jax.ShapeDtypeStruct((4, *cells), jnp.float32),
-        ],
+        out_shape=[vmem(16, 2, 2, 8, LANES)] + [vmem(2, 4, 8, LANES)] * 3,
         scratch_shapes=[pltpu.VMEM((5, 8, LANES), jnp.float32)],
         name="pencil",
     )(
-        received.reshape(16, 2, 2, 8, LANES),
+        near(received.reshape(16, 2, 2, 8, LANES)),
         filter_matrices[0],
-        partial,
-        velocity,
-        before,
-        after,
-        other_edge,
+        near(ends),
+        near(before),
+        near(after),
         dilatation_bin,
         vorticity_bin,
         shock_switch,
+        near(counts),
     )
     received = lax.all_to_all(send.reshape(32, 16, LANES), ("gx", "gy"), 0, 0, tiled=True)
     scale = HISTOGRAM_BINS * HISTOGRAM_BINS / (cells_x * slabs * span * total_y)
     conserved_next, histogram = pl.pallas_call(
         lambda *refs: final_kernel(scale, *refs),
-        out_shape=[
-            jax.ShapeDtypeStruct((5, cells_x, span, cells_y), jnp.float32),
-            jax.ShapeDtypeStruct((HISTOGRAM_BINS, HISTOGRAM_BINS), jnp.float32),
-        ],
+        out_shape=[f32(5, cells_x, span, cells_y), f32(HISTOGRAM_BINS, HISTOGRAM_BINS)],
         scratch_shapes=[pltpu.VMEM((72, LANES), jnp.float32)],
         name="final",
-    )(received.reshape(512, LANES), updated, updated_energy, weight)
+    )(*map(near, (received.reshape(512, LANES), updated, updated_energy, weight, *end_rows)))
     return (conserved_next, histogram)
 
 

time: 44 us -> 40.3 us (0.916)
  waiting for transfers between devices: 5.37 us -> 3.27 us
  local copies, waits for them, and re-layouts: 0.71 us -> 0 us
  Pallas kernels: 8.85 us -> 8.22 us
    ppermute x1, waiting for transfers between devices: 4.22 us -> 2.24 us  [shards(): after = lax.ppermute(first, 'gx', down)]
    unnamed x14 -> x0, local copies, waits for them, and re-layouts: 0.71 us -> none
    pallas_call x3 -> x4, Pallas kernels: 8.85 us -> 8.22 us  [the longest x1 2.64 us: shards(): pl.pallas_call(lambda *refs: slab_kernel(amplitude, *refs), out_shape=[vm...]
  transfers between devices with their start and end apart: 4 -> 4, of which waited for: 3 -> 2; matrix products, arithmetic and copies ran while one was open for 0% -> 0% of each run, Pallas kernels for 0% -> 5%
where the time goes in v2:
time: 40.3 us; the launch traced here: 40 us
  blocking collectives  15.4 us (38%)
  starting transfers between devices  12.5 us (31%)
  Pallas kernels  8.22 us (20%)
  waiting for transfers between devices  3.27 us (8%)
  between operations  0.69 us (2%)
    all_to_all x1, blocking collectives, shards(): lax.all_to_all(send.reshape(32, 16, LANES), ('gx', 'gy'), 0, 0, tiled=True)  15.4 us
    all_to_all x1, starting transfers between devices, shards(): lax.all_to_all(send.reshape(32, 16, LANES), ('gx', 'gy'), 0, 0, tiled=True)  7.3 us
    ppermute x1, starting transfers between devices, shards(): before = lax.ppermute(last, 'gx', up)  3.57 us
    pallas_call x1, Pallas kernels, shards(): pl.pallas_call(lambda *refs: slab_kernel(amplitude, *refs), out_shape=[vm...  2.64 us
    pallas_call x1, Pallas kernels, shards(): pl.pallas_call(pencil_kernel, out_shape=[vmem(16, 2, 2, 8, LANES)] + [vme...  2.34 us
    ppermute x1, waiting for transfers between devices, shards(): after = lax.ppermute(first, 'gx', down)  2.24 us
    pallas_call x1, Pallas kernels, shards(): pl.pallas_call(interior_kernel, out_shape=[vmem(4, *cells), vmem(4, *cell...  2.11 us
    ppermute x1, starting transfers between devices, shards(): after = lax.ppermute(first, 'gx', down)  1.29 us
  transfers between devices with their start and end apart: 4, of which 2 were waited for; matrix products, arithmetic and copies ran while one was open for 0% of the time, Pallas kernels for 5%

profile of v2, /device:TPU:0, one launch (start us, length us, event | category | flops | bytes accessed | tf_op | source)
XLA Modules:
  0.0 40.0 jit_solution(8811050283708644394)
XLA Ops:
  0.6 2.6 %slab.1 = (f32[512,128]{1,0:T(8,128)}, f32[5,8,128]{2,1,0:T(8,128)S(1)}, f32[5,8,128]{2,1,0:T(8,128)S(1)}, f32[8,8,128]{2,1,0:T(8,128)S(1)}) custom-call(f32[8,32,32]{2,1,0:T(8,128)} %density.1, f32[3,8,32,32]{3,2,1,0:T(8,128)} %momentum.1, f32[8,32,32]{2,1,0:T(8,128)} %energy.1, s32[1,64]{1,0:T(1,128)} %bitcast.14, s32[1,64]{1,0:T(1,128)} %bitcast.15, ...), custom_call_target="tpu_custom_call" | custom-call | tf_op jit(solution)/shard_map/slab/pallas_call | solution.py:670
  3.3 7.3 %all-to-all-start = ((f32[32,16,128]{2,1,0:T(8,128)}), f32[32,16,128]{2,1,0:T(8,128)S(1)}, u32[]{:S(2)}, u32[]{:S(2)}) async-start(f32[32,16,128]{2,1,0:T(8,128)} %bitcast.4), calls=%async_computation | async-start | bytes 524288 | tf_op jit(solution)/shard_map/all_to_all | solution.py:683
  10.6 0.3 collective-permute-start
  10.9 3.6 %collective-permute-start.1 = (f32[5,8,128]{2,1,0:T(8,128)S(1)}, f32[5,8,128]{2,1,0:T(8,128)S(1)}, u32[]{:S(2)}, u32[]{:S(2)}) collective-permute-start(f32[5,8,128]{2,1,0:T(8,128)S(1)} %get-tuple-element.18), channel_id=1, source_target_pairs={{0,2},{2,4},{4,6},{6,8},{8,10},{10,12},{12,14},{14,16},{16,18},{18... | collective-permute-start | bytes 61448 | tf_op jit(solution)/shard_map/ppermute | solution.py:686
  14.5 1.3 %collective-permute-start.2 = (f32[5,8,128]{2,1,0:T(8,128)S(1)}, f32[5,8,128]{2,1,0:T(8,128)S(1)}, u32[]{:S(2)}, u32[]{:S(2)}) collective-permute-start(f32[5,8,128]{2,1,0:T(8,128)S(1)} %get-tuple-element.19), channel_id=1, source_target_pairs={{2,0},{4,2},{6,4},{8,6},{10,8},{12,10},{14,12},{16,14},{18,16},{20... | collective-permute-start | bytes 61448 | tf_op jit(solution)/shard_map/ppermute | solution.py:687
  15.8 0.0 collective-permute-done.edge
  15.8 2.1 %interior.1 = (f32[4,8,8,128]{3,2,1,0:T(8,128)S(1)}, f32[4,8,8,128]{3,2,1,0:T(8,128)S(1)}, f32[4,8,8,128]{3,2,1,0:T(8,128)S(1)}, f32[9,2,8,128]{3,2,1,0:T(8,128)S(1)}, f32[8,64]{1,0:T(8,128)S(1)}) custom-call(f32[8,32,32]{2,1,0:T(8,128)} %density.1, f32[3,8,32,32]{3,2,1,0:T(8,128)} %momentum.1, f32[8,32,32]{2,1,0:T(8,128)} %energy.1, ...), custom_call_target="tpu_custom_call" | custom-call | flops 10000000 | bytes 2000000 | tf_op jit(solution)/shard_map/interior/pallas_call | solution.py:689
  17.9 0.0 collective-permute-done.1.before
  17.9 2.2 %collective-permute-done.2.after = f32[5,8,128]{2,1,0:T(8,128)S(1)} collective-permute-done((f32[5,8,128]{2,1,0:T(8,128)S(1)}, f32[5,8,128]{2,1,0:T(8,128)S(1)}, u32[]{:S(2)}, u32[]{:S(2)}) %collective-permute-start.2) | collective-permute-done | bytes 20512 | tf_op jit(solution)/shard_map/ppermute | solution.py:687
  20.2 1.0 %all-to-all-done = f32[32,16,128]{2,1,0:T(8,128)S(1)} async-done(((f32[32,16,128]{2,1,0:T(8,128)}), f32[32,16,128]{2,1,0:T(8,128)S(1)}, u32[]{:S(2)}, u32[]{:S(2)}) %all-to-all-start) | async-done | bytes 262176 | tf_op jit(solution)/shard_map/all_to_all | solution.py:683
  21.2 2.3 %pencil.1 = (f32[16,2,2,8,128]{4,3,2,1,0:T(8,128)S(1)}, f32[2,4,8,128]{3,2,1,0:T(8,128)S(1)}, f32[2,4,8,128]{3,2,1,0:T(8,128)S(1)}, f32[2,4,8,128]{3,2,1,0:T(8,128)S(1)}) custom-call(f32[16,2,2,8,128]{4,3,2,1,0:T(8,128)S(1)} %bitcast.10, f32[128,128]{1,0:T(8,128)} %bitcast.12, f32[9,2,8,128]{3,2,1,0:T(8,128)S(1)} %get-tuple-element.17.ends, ...), custom_call_target="tpu_custom_call" | custom-call | tf_op jit(solution)/shard_map/pencil/pallas_call | solution.py:695
  23.5 15.4 %all_to_all.10 = f32[32,16,128]{2,1,0:T(8,128)S(1)} all-to-all(f32[32,16,128]{2,1,0:T(8,128)S(1)} %bitcast.11), channel_id=1, replica_groups=mesh['gx'=16,'gy'=2] {'gx','gy'}, dimensions={0} | all-to-all | bytes 524288 | tf_op jit(solution)/shard_map/all_to_all | solution.py:711
  38.9 1.1 %final.1 = (f32[5,8,32,32]{3,2,1,0:T(8,128)}, f32[64,64]{1,0:T(8,128)}) custom-call(f32[512,128]{1,0:T(8,128)S(1)} %bitcast.9, f32[4,8,8,128]{3,2,1,0:T(8,128)S(1)} %get-tuple-element.22.refs_1_, f32[4,8,8,128]{3,2,1,0:T(8,128)S(1)} %get-tuple-element.23.refs_2_, f32[4,8,8,128]{3,2,1,0:T(8,128)S(1)} %get-tuple-element.24.refs_3_, ...), custom_call_target="tpu_custom_call" | custom-call | tf_op jit(solution)/shard_map/final/pallas_call | solution.py:713
Async XLA Ops:
  3.3 17.9 %all-to-all-start = ((f32[32,16,128]{2,1,0:T(8,128)}), f32[32,16,128]{2,1,0:T(8,128)S(1)}, u32[]{:S(2)}, u32[]{:S(2)}) async-start(f32[32,16,128]{2,1,0:T(8,128)} %bitcast.4), calls=%async_computation | async-start | bytes 524288 | tf_op jit(solution)/shard_map/all_to_all | solution.py:683
  10.6 5.2 %collective-permute-start = (f32[8,8,128]{2,1,0:T(8,128)S(1)}, f32[8,8,128]{2,1,0:T(8,128)S(1)}, u32[]{:S(2)}, u32[]{:S(2)}) collective-permute-start(f32[8,8,128]{2,1,0:T(8,128)S(1)} %get-tuple-element.16), channel_id=1, source_target_pairs={{0,1},{1,0},{2,3},{3,2},{4,5},{5,4},{6,7},{7,6},{8,9},{9,8},{10,11... | collective-permute-start | bytes 98312 | tf_op jit(solution)/shard_map/ppermute | solution.py:688
  10.9 7.0 %collective-permute-start.1 = (f32[5,8,128]{2,1,0:T(8,128)S(1)}, f32[5,8,128]{2,1,0:T(8,128)S(1)}, u32[]{:S(2)}, u32[]{:S(2)}) collective-permute-start(f32[5,8,128]{2,1,0:T(8,128)S(1)} %get-tuple-element.18), channel_id=1, source_target_pairs={{0,2},{2,4},{4,6},{6,8},{8,10},{10,12},{12,14},{14,16},{16,18},{18... | collective-permute-start | bytes 61448 | tf_op jit(solution)/shard_map/ppermute | solution.py:686
  14.5 5.7 %collective-permute-start.2 = (f32[5,8,128]{2,1,0:T(8,128)S(1)}, f32[5,8,128]{2,1,0:T(8,128)S(1)}, u32[]{:S(2)}, u32[]{:S(2)}) collective-permute-start(f32[5,8,128]{2,1,0:T(8,128)S(1)} %get-tuple-element.19), channel_id=1, source_target_pairs={{2,0},{4,2},{6,4},{8,6},{10,8},{12,10},{14,12},{16,14},{18,16},{20... | collective-permute-start | bytes 61448 | tf_op jit(solution)/shard_map/ppermute | solution.py:687

commit v3 on v2

--- a/solution.py
+++ b/solution.py
@@ -268,12 +268,13 @@
     signs,
     strengths,
     send,
-    first_out,
-    last_out,
+    far_out,
+    pair_out,
     edge_out,
 ):
     slab = lax.axis_index("gx")
     first_core = lax.axis_index("gy") == 0
+    odd = slab % 2 == 1
     last_slab = slab == lax.axis_size("gx") - 1
     q = [packed(density)] + [packed(momentum, c) for c in range(3)] + [packed(energy)]
     vel, pressure = velocity_pressure(q)
@@ -288,8 +289,8 @@
         change = change + y_difference(flux_y[f], first_core)
         change = change + z_difference(flux_z[f])
         partial.append(q[f] - HALF_STEP * change)
-        first_out[f] = q[f][0]
-        last_out[f] = q[f][7]
+        far_out[f] = jnp.where(odd, q[f][7], q[f][0])
+        pair_out[f] = jnp.where(odd, q[f][0], q[f][7])
 
     lane = iota((8, 8, LANES), 2) % 32
     edge = jnp.zeros((8, 8, LANES), jnp.float32)
@@ -377,10 +378,9 @@
     return counts[:8] + counts[8:]
 
 
-def slab_bins(vorticity_bin, rows):
-    slab = lax.axis_index("gx")
-    base = slab * HISTOGRAM_BINS // lax.axis_size("gx")
-    return (packed(vorticity_bin, rows) - base) & (HISTOGRAM_BINS - 1)
+def slab_bins(bins):
+    base = lax.axis_index("gx") * HISTOGRAM_BINS // lax.axis_size("gx")
+    return (bins - base) & (HISTOGRAM_BINS - 1)
 
 
 def interior_kernel(
@@ -391,11 +391,15 @@
     dilatation_bin,
     vorticity_bin,
     switch,
+    matrix,
     updated_out,
     energy_out,
     weight_out,
     ends_out,
     counts_out,
+    bins_out,
+    matrix_out,
+    mask_out,
 ):
     first_core = lax.axis_index("gy") == 0
     last_slab = lax.axis_index("gx") == lax.axis_size("gx") - 1
@@ -434,38 +438,44 @@
         ends_out[i, 0] = a[0]
         ends_out[i, 1] = a[7]
     dil = packed(dilatation_bin)
-    vort = slab_bins(vorticity_bin, slice(None))
+    vort = slab_bins(packed(vorticity_bin))
     inner = range(1, 7)
     counts_out[...] = counted(
         [sensor[x] for x in inner], [dil[x] for x in inner], [vort[x] for x in inner]
     )
+    for end in range(2):
+        bins_out[0, end] = dil[7 * end]
+        bins_out[1, end] = vort[7 * end]
+    matrix_out[0], matrix_out[1] = halves(matrix[...])
+    mask_out[...] = jnp.broadcast_to(mask, (8, LANES))
 
 
 def pencil_kernel(
     received,
     matrix,
     ends,
-    before,
-    after,
-    dilatation_bin,
-    vorticity_bin,
-    switch,
     counts_in,
+    bins,
+    mask,
+    far,
+    pair,
     send,
     updated_out,
     energy_out,
     weight_out,
-    ghost_planes,
+    before,
 ):
     slab = lax.axis_index("gx")
     core = lax.axis_index("gy")
     last_slab = slab == lax.axis_size("gx") - 1
+    odd = slab % 2 == 1
     plane = (slab * 2 + core).astype(jnp.float32)
     row = iota((8, LANES), 0)
     lane = iota((8, LANES), 1)
     peak = HAT_PEAK * HAT_PEAK
 
-    tiles = [[received[g, h, 1] for g in range(16)] for h in range(2)]
+    chunk_tile = lambda g, h, t: received[pl.ds(32 * g + 16 * h + 8 * t, 8), :]
+    tiles = [[chunk_tile(g, h, 1) for g in range(16)] for h in range(2)]
     chunks = []
     for h in range(2):
         for a in range(4):
@@ -505,25 +515,22 @@
         ]
         q = ghost_state_rows(*parts)
         for f in range(5):
-            ghost_planes[f] = q[f]
+            before[f] = q[f]
 
     @pl.when(slab != 0)
     def _():
-        ghost_planes[...] = before[...]
-
-    face_a, face_e = [], []
-    for h in range(2):
-        fa, fe = [], []
-        for g in range(16):
-            tile = tiles[h][g]
-            out = None
-            for f in range(4):
-                moved = roll(roll(tile, 32 * (f - 3), 1), -2 * f, 0)
-                out = moved if out is None else jnp.where(lane // 32 == f, moved, out)
-            fa.append(out)
-            fe.append(roll(tile, -32, 1))
-        face_a.append(fa)
-        face_e.append(fe)
+        before[...] = jnp.where(odd, pair[...], far[...])
+
+    chunk_row = lambda r: received[pl.ds(8 + r, 32, stride=16), :]
+    group = iota((32, LANES), 1) // 32
+    faces = []
+    for slots in ((0, 2, 4, 6), (7, 1, 3, 5)):
+        side = None
+        for f, r in enumerate(slots):
+            moved = roll(chunk_row(r), 32 * (f - 3), 1)
+            side = moved if side is None else jnp.where(group == f, moved, side)
+        faces.append((side, roll(chunk_row(slots[0]), -32, 1)))
+    last_faces, first_faces = faces
     columns_a, columns_e = [], []
     for h in range(2):
         own = slice(32 * h, 32 * h + 32)
@@ -531,9 +538,14 @@
         ghost_e = jnp.concatenate([ghost_x[4][:, own]] * 4, axis=1)
         ca, ce = [], []
         for g in range(16):
-            zero = jnp.zeros((8, LANES), jnp.float32)
-            previous_a, previous_e = (face_a[h][g - 1], face_e[h][g - 1]) if g else (ghost_a, ghost_e)
-            next_a, next_e = (face_a[h][g + 1], face_e[h][g + 1]) if g < 15 else (zero, zero)
+            zero = jnp.zeros((1, LANES), jnp.float32)
+            i, j = 2 * g + h - 2, 2 * g + h + 2
+            previous_a, previous_e = ghost_a, ghost_e
+            if g > 0:
+                previous_a, previous_e = last_faces[0][i : i + 1], last_faces[1][i : i + 1]
+            next_a, next_e = zero, zero
+            if g < 15:
+                next_a, next_e = first_faces[0][j : j + 1], first_faces[1][j : j + 1]
             fix_a = jnp.where(row == 0, previous_a, jnp.where(row == 7, -next_a, 0.0))
             fix_e = jnp.where(row == 0, previous_e, jnp.where(row == 7, -next_e, 0.0))
             other = tiles[1 - h][g]
@@ -544,14 +556,14 @@
                 fix_a = jnp.where(lane == 32 * f + target, fix_a + side * moved, fix_a)
             moved = roll(other, target - 68, 1)
             fix_e = jnp.where(lane == target, fix_e + side * moved, fix_e)
-            ca.append(received[g, h, 0] + HALF_STEP * fix_a)
+            ca.append(chunk_tile(g, h, 0) + HALF_STEP * fix_a)
             ce.append(jnp.where(lane < 32, tiles[h][g] + HALF_STEP * fix_e, 0.0))
         columns_a.append(jnp.concatenate(ca, axis=0))
         columns_e.append(jnp.concatenate(ce, axis=0))
     columns = jnp.concatenate(
         [columns_a[0], columns_a[1], columns_e[0] + roll(columns_e[1], 32, 1)], axis=1
     )
-    m_high, m_low = halves(matrix[...])
+    m_high, m_low = matrix[0], matrix[1]
     c_high, c_low = halves(columns)
     smooth = (
         jnp.dot(m_high, c_high, preferred_element_type=jnp.float32)
@@ -560,9 +572,8 @@
     )
 
     sensors, dils, vorts = [], [], []
-    mask = jnp.concatenate([switch[...].astype(jnp.float32)] * 4, axis=1)
-    for end, ref in ((0, ghost_planes), (1, after)):
-        q = [ref[f] for f in range(5)]
+    for end in range(2):
+        q = [jnp.where(odd, far[f], pair[f]) if end else before[f] for f in range(5)]
         vel, pressure = velocity_pressure(q)
         flux = euler_flux(q, vel, pressure, 0)
         sign = -1.0 if end == 0 else 1.0
@@ -573,15 +584,14 @@
         rates = [ends[5 + i, end] for i in range(4)]
         rates = [rates[0] + add[5], rates[1], rates[2] - add[7], rates[3] + add[6]]
         sensor = sensor_of(*rates)
-        weight = sensor * mask
+        weight = sensor * mask[...]
         for k in range(4):
             updated_out[end, k] = regrouped(updated[:4], k)
             energy_out[end, k] = roll(updated[4], -32 * k, 1)
             weight_out[end, k] = regrouped([weight] * 4, k)
-        at = pl.ds(7 * end, 1)
         sensors.append(sensor)
-        dils.append(packed(dilatation_bin, at)[0])
-        vorts.append(slab_bins(vorticity_bin, at)[0])
+        dils.append(bins[0, end])
+        vorts.append(bins[1, end])
     counts = counts_in[...] + counted(sensors, dils, vorts)
     counts = jnp.concatenate([jnp.zeros((8, 64), jnp.float32), counts], axis=1)
 
@@ -667,7 +677,7 @@
     f32 = lambda *shape: jax.ShapeDtypeStruct(shape, jnp.float32)
     vmem = lambda *shape: pltpu.VMEM(shape, jnp.float32)
     near = lambda a: pltpu.with_memory_space_constraint(a, pltpu.VMEM)
-    send, first, last, edge = pl.pallas_call(
+    send, far, pair, edge = pl.pallas_call(
         lambda *refs: slab_kernel(amplitude, *refs),
         out_shape=[vmem(512, LANES), vmem(5, 8, LANES), vmem(5, 8, LANES), vmem(*cells)],
         name="slab",
@@ -681,32 +691,42 @@
         eddy_strengths.reshape(1, -1),
     )
     received = lax.all_to_all(send.reshape(32, 16, LANES), ("gx", "gy"), 0, 0, tiled=True)
-    up = [(i, i + 1) for i in range(slabs - 1)]
-    down = [(j, i) for i, j in up]
-    before = lax.ppermute(last, "gx", up)
-    after = lax.ppermute(first, "gx", down)
+    both = lambda first: [p for i in range(first, slabs - 1, 2) for p in ((i, i + 1), (i + 1, i))]
+    far = lax.ppermute(far, "gx", both(1))
+    pair = lax.ppermute(pair, "gx", both(0))
     other_edge = lax.ppermute(edge, "gy", [(0, 1), (1, 0)])
-    updated, updated_energy, weight, ends, counts = pl.pallas_call(
+    updated, updated_energy, weight, ends, counts, bins, matrix, mask = pl.pallas_call(
         interior_kernel,
-        out_shape=[vmem(4, *cells), vmem(4, *cells), vmem(4, *cells), vmem(9, 2, 8, LANES), vmem(8, 64)],
+        out_shape=[
+            vmem(4, *cells),
+            vmem(4, *cells),
+            vmem(4, *cells),
+            vmem(9, 2, 8, LANES),
+            vmem(8, 64),
+            pltpu.VMEM((2, 2, 8, LANES), jnp.int32),
+            pltpu.VMEM((2, *filter_matrices.shape[1:]), jnp.bfloat16),
+            vmem(8, LANES),
+        ],
         cost_estimate=pl.CostEstimate(flops=10_000_000, bytes_accessed=2_000_000, transcendentals=0),
         name="interior",
-    )(density, momentum, energy, near(other_edge), dilatation_bin, vorticity_bin, shock_switch)
+    )(
+        density,
+        momentum,
+        energy,
+        near(other_edge),
+        dilatation_bin,
+        vorticity_bin,
+        shock_switch,
+        filter_matrices[0],
+    )
     send, *end_rows = pl.pallas_call(
         pencil_kernel,
         out_shape=[vmem(16, 2, 2, 8, LANES)] + [vmem(2, 4, 8, LANES)] * 3,
         scratch_shapes=[pltpu.VMEM((5, 8, LANES), jnp.float32)],
         name="pencil",
     )(
-        near(received.reshape(16, 2, 2, 8, LANES)),
-        filter_matrices[0],
-        near(ends),
-        near(before),
-        near(after),
-        dilatation_bin,
-        vorticity_bin,
-        shock_switch,
-        near(counts),
+        near(received.reshape(512, LANES)),
+        *map(near, (matrix, ends, counts, bins, mask, far, pair)),
     )
     received = lax.all_to_all(send.reshape(32, 16, LANES), ("gx", "gy"), 0, 0, tiled=True)
     scale = HISTOGRAM_BINS * HISTOGRAM_BINS / (cells_x * slabs * span * total_y)

time: 40.3 us -> 36.5 us (0.906)
  blocking collectives: 15.4 us -> 12.6 us
  Pallas kernels: 8.22 us -> 7.19 us
    all_to_all x1, blocking collectives: 15.4 us -> 12.6 us  [shards(): lax.all_to_all(send.reshape(32, 16, LANES), ('gx', 'gy'), 0, 0, tiled=True)]
    ppermute x2, waiting for transfers between devices: 2.24 us -> 0.01 us  [the longest x1 0.01 us: shards(): far = lax.ppermute(far, 'gx', both(1))]
    all_to_all x1, waiting for transfers between devices: 1.02 us -> 3.01 us  [shards(): lax.all_to_all(send.reshape(32, 16, LANES), ('gx', 'gy'), 0, 0, tiled=True)]
    pallas_call x1, Pallas kernels: 2.34 us -> 1.31 us  [shards(): pl.pallas_call(pencil_kernel, out_shape=[vmem(16, 2, 2, 8, LANES)] + [vme...]
  transfers between devices with their start and end apart: 4 -> 4, of which waited for: 2 -> 1; matrix products, arithmetic and copies ran while one was open for 0% -> 0% of each run, Pallas kernels for 5% -> 6%
where the time goes in v3:
time: 36.5 us; the launch traced here: 36.2 us
  starting transfers between devices  12.7 us (35%)
  blocking collectives  12.6 us (35%)
  Pallas kernels  7.19 us (20%)
  waiting for transfers between devices  3.02 us (8%)
  between operations  0.68 us (2%)
    all_to_all x1, blocking collectives, shards(): lax.all_to_all(send.reshape(32, 16, LANES), ('gx', 'gy'), 0, 0, tiled=True)  12.6 us
    all_to_all x1, starting transfers between devices, shards(): lax.all_to_all(send.reshape(32, 16, LANES), ('gx', 'gy'), 0, 0, tiled=True)  7.3 us
    ppermute x1, starting transfers between devices, shards(): pair = lax.ppermute(pair, 'gx', both(0))  4.45 us
    all_to_all x1, waiting for transfers between devices, shards(): lax.all_to_all(send.reshape(32, 16, LANES), ('gx', 'gy'), 0, 0, tiled=True)  3.01 us
    pallas_call x1, Pallas kernels, shards(): pl.pallas_call(lambda *refs: slab_kernel(amplitude, *refs), out_shape=[vm...  2.64 us
    pallas_call x1, Pallas kernels, shards(): pl.pallas_call(interior_kernel, out_shape=[vmem(4, *cells), vmem(4, *cell...  2.13 us
    pallas_call x1, Pallas kernels, shards(): pl.pallas_call(pencil_kernel, out_shape=[vmem(16, 2, 2, 8, LANES)] + [vme...  1.31 us
    pallas_call x1, Pallas kernels, shards(): pl.pallas_call(lambda *refs: final_kernel(scale, *refs), out_shape=[f32(5...  1.11 us
  transfers between devices with their start and end apart: 4, of which 1 were waited for; matrix products, arithmetic and copies ran while one was open for 0% of the time, Pallas kernels for 6%

profile of v3, /device:TPU:0, one launch (start us, length us, event | category | flops | bytes accessed | tf_op | source)
XLA Modules:
  0.0 36.2 jit_solution(10979088687580509883)
XLA Ops:
  0.6 2.6 %slab.1 = (f32[512,128]{1,0:T(8,128)}, f32[5,8,128]{2,1,0:T(8,128)S(1)}, f32[5,8,128]{2,1,0:T(8,128)S(1)}, f32[8,8,128]{2,1,0:T(8,128)S(1)}) custom-call(f32[8,32,32]{2,1,0:T(8,128)} %density.1, f32[3,8,32,32]{3,2,1,0:T(8,128)} %momentum.1, f32[8,32,32]{2,1,0:T(8,128)} %energy.1, s32[1,64]{1,0:T(1,128)} %bitcast.14, s32[1,64]{1,0:T(1,128)} %bitcast.15, ...), custom_call_target="tpu_custom_call" | custom-call | tf_op jit(solution)/shard_map/slab/pallas_call | solution.py:680
  3.3 7.3 %all-to-all-start = ((f32[32,16,128]{2,1,0:T(8,128)}), f32[32,16,128]{2,1,0:T(8,128)S(1)}, u32[]{:S(2)}, u32[]{:S(2)}) async-start(f32[32,16,128]{2,1,0:T(8,128)} %bitcast.4), calls=%async_computation | async-start | bytes 524288 | tf_op jit(solution)/shard_map/all_to_all | solution.py:693
  10.6 0.3 collective-permute-start
  10.9 0.7 %collective-permute-start.1 = (f32[5,8,128]{2,1,0:T(8,128)S(1)}, f32[5,8,128]{2,1,0:T(8,128)S(1)}, u32[]{:S(2)}, u32[]{:S(2)}) collective-permute-start(f32[5,8,128]{2,1,0:T(8,128)S(1)} %get-tuple-element.25), channel_id=1, source_target_pairs={{2,4},{4,2},{6,8},{8,6},{10,12},{12,10},{14,16},{16,14},{18,20},{2... | collective-permute-start | bytes 61448 | tf_op jit(solution)/shard_map/ppermute | solution.py:695
  11.6 4.5 %collective-permute-start.2 = (f32[5,8,128]{2,1,0:T(8,128)S(1)}, f32[5,8,128]{2,1,0:T(8,128)S(1)}, u32[]{:S(2)}, u32[]{:S(2)}) collective-permute-start(f32[5,8,128]{2,1,0:T(8,128)S(1)} %get-tuple-element.26), channel_id=1, source_target_pairs={{0,2},{2,0},{4,6},{6,4},{8,10},{10,8},{12,14},{14,12},{16,18},{18,... | collective-permute-start | bytes 61448 | tf_op jit(solution)/shard_map/ppermute | solution.py:696
  16.0 0.0 collective-permute-done.edge
  16.0 2.1 %interior.1 = (f32[4,8,8,128]{3,2,1,0:T(8,128)S(1)}, f32[4,8,8,128]{3,2,1,0:T(8,128)S(1)}, f32[4,8,8,128]{3,2,1,0:T(8,128)S(1)}, f32[9,2,8,128]{3,2,1,0:T(8,128)...) custom-call(f32[8,32,32]{2,1,0:T(8,128)} %density.1, ...), custom_call_target="tpu_custom_call" | custom-call | flops 10000000 | bytes 2000000 | tf_op jit(solution)/shard_map/interior/pallas_call | solution.py:698
  18.1 0.0 collective-permute-done.1.far
  18.2 0.0 collective-permute-done.2.pair
  18.2 3.0 %all-to-all-done = f32[32,16,128]{2,1,0:T(8,128)S(1)} async-done(((f32[32,16,128]{2,1,0:T(8,128)}), f32[32,16,128]{2,1,0:T(8,128)S(1)}, u32[]{:S(2)}, u32[]{:S(2)}) %all-to-all-start) | async-done | bytes 262176 | tf_op jit(solution)/shard_map/all_to_all | solution.py:693
  21.2 1.3 %pencil.1 = (f32[16,2,2,8,128]{4,3,2,1,0:T(8,128)S(1)}, f32[2,4,8,128]{3,2,1,0:T(8,128)S(1)}, f32[2,4,8,128]{3,2,1,0:T(8,128)S(1)}, f32[2,4,8,128]{3,2,1,0:T(8,128)S(1)}) custom-call(f32[512,128]{1,0:T(8,128)S(1)} %bitcast.10, bf16[2,128,128]{2,1,0:T(8,128)(2,1)S(1)} %get-tuple-element.20.matrix, f32[9,2,8,128]{3,2,1,0:T(8,128)S(1)} %get-tuple-element.21.ends, ...), custom_call_target="tpu_custom_call" | custom-call | tf_op jit(solution)/shard_map/pencil/pallas_call | solution.py:722
  22.5 12.6 %all_to_all.10 = f32[32,16,128]{2,1,0:T(8,128)S(1)} all-to-all(f32[32,16,128]{2,1,0:T(8,128)S(1)} %bitcast.11), channel_id=1, replica_groups=mesh['gx'=16,'gy'=2] {'gx','gy'}, dimensions={0} | all-to-all | bytes 524288 | tf_op jit(solution)/shard_map/all_to_all | solution.py:731
  35.1 1.1 %final.1 = (f32[5,8,32,32]{3,2,1,0:T(8,128)}, f32[64,64]{1,0:T(8,128)}) custom-call(f32[512,128]{1,0:T(8,128)S(1)} %bitcast.9, f32[4,8,8,128]{3,2,1,0:T(8,128)S(1)} %get-tuple-element.28.refs_1_, f32[4,8,8,128]{3,2,1,0:T(8,128)S(1)} %get-tuple-element.29.refs_2_, f32[4,8,8,128]{3,2,1,0:T(8,128)S(1)} %get-tuple-element.30.refs_3_, ...), custom_call_target="tpu_custom_call" | custom-call | tf_op jit(solution)/shard_map/final/pallas_call | solution.py:733
Async XLA Ops:
  3.3 17.9 %all-to-all-start = ((f32[32,16,128]{2,1,0:T(8,128)}), f32[32,16,128]{2,1,0:T(8,128)S(1)}, u32[]{:S(2)}, u32[]{:S(2)}) async-start(f32[32,16,128]{2,1,0:T(8,128)} %bitcast.4), calls=%async_computation | async-start | bytes 524288 | tf_op jit(solution)/shard_map/all_to_all | solution.py:693
  10.6 5.4 %collective-permute-start = (f32[8,8,128]{2,1,0:T(8,128)S(1)}, f32[8,8,128]{2,1,0:T(8,128)S(1)}, u32[]{:S(2)}, u32[]{:S(2)}) collective-permute-start(f32[8,8,128]{2,1,0:T(8,128)S(1)} %get-tuple-element.19), channel_id=1, source_target_pairs={{0,1},{1,0},{2,3},{3,2},{4,5},{5,4},{6,7},{7,6},{8,9},{9,8},{10,11... | collective-permute-start | bytes 98312 | tf_op jit(solution)/shard_map/ppermute | solution.py:697
  10.9 7.3 %collective-permute-start.1 = (f32[5,8,128]{2,1,0:T(8,128)S(1)}, f32[5,8,128]{2,1,0:T(8,128)S(1)}, u32[]{:S(2)}, u32[]{:S(2)}) collective-permute-start(f32[5,8,128]{2,1,0:T(8,128)S(1)} %get-tuple-element.25), channel_id=1, source_target_pairs={{2,4},{4,2},{6,8},{8,6},{10,12},{12,10},{14,16},{16,14},{18,20},{2... | collective-permute-start | bytes 61448 | tf_op jit(solution)/shard_map/ppermute | solution.py:695
  11.6 6.6 %collective-permute-start.2 = (f32[5,8,128]{2,1,0:T(8,128)S(1)}, f32[5,8,128]{2,1,0:T(8,128)S(1)}, u32[]{:S(2)}, u32[]{:S(2)}) collective-permute-start(f32[5,8,128]{2,1,0:T(8,128)S(1)} %get-tuple-element.26), channel_id=1, source_target_pairs={{0,2},{2,0},{4,6},{6,4},{8,10},{10,8},{12,14},{14,12},{16,18},{18,... | collective-permute-start | bytes 61448 | tf_op jit(solution)/shard_map/ppermute | solution.py:696

commit v4 on v3

--- a/solution.py
+++ b/solution.py
@@ -196,6 +196,8 @@
 
 
 LANES = 128
+SENT = 15
+BACK = 13
 HALF_STEP = 0.5 * TIME_STEP
 
 
@@ -292,44 +294,36 @@
         far_out[f] = jnp.where(odd, q[f][7], q[f][0])
         pair_out[f] = jnp.where(odd, q[f][0], q[f][7])
 
-    lane = iota((8, 8, LANES), 2) % 32
-    edge = jnp.zeros((8, 8, LANES), jnp.float32)
+    lane2 = iota((8, LANES), 1)
+    shift = jnp.where(first_core, LANES - 31, 0)
+    sides = []
     for i, value in enumerate(flux_y + vel):
-        near = jnp.where(first_core, roll(value, i - 31, 2), roll(value, i, 2))
-        edge = jnp.where(lane == i, near, edge)
-    edge_out[...] = edge
-
-    own = slice(0, 32), slice(32, 64)
-    pick = lambda a: jnp.where(first_core, a[:, own[0]], a[:, own[1]])
+        side = jnp.zeros((8, LANES), jnp.float32)
+        for x in range(8):
+            side = jnp.where(lane2 % 32 == x, pltpu.roll(value[x], shift + x, 1), side)
+        edge_out[i] = side
+        sides.append(side)
+    energy_side = roll(sides[4], 8, 1)
+    sides = [jnp.where(lane2 % 32 < 8, sides[0], energy_side)] + sides[1:4]
+
+    pick = lambda a: jnp.where(first_core, a[:, :32], a[:, 32:])
     strength = strengths[...] * amplitude
-    rows = [pick(normal_cell[...]).astype(jnp.float32), pick(spanwise_cell[...]).astype(jnp.float32)]
+    eddies = [pick(normal_cell[...]).astype(jnp.float32), pick(spanwise_cell[...]).astype(jnp.float32)]
     for c in range(3):
         sign = (2 * signs[c : c + 1, :] - 1).astype(jnp.float32)
-        rows.append(pick(sign * strength))
-    blank = jnp.zeros((1, 32), jnp.float32)
-    eddies = jnp.concatenate([blank] + rows + [blank, blank], axis=0)
-    eddies = jnp.concatenate([eddies] * 4, axis=1)
-
-    slots = [flux_x[4][7], None, None, None, None, None, None, flux_x[4][0]]
-    extra = jnp.stack([eddies if s is None else s for s in slots])
-    faces = [None] * 8
-    for f in range(4):
-        faces[2 * f] = flux_x[f][7]
-        faces[(2 * f - 1) % 8] = flux_x[f][0]
-    faces = jnp.stack(faces)
-    row = iota((8, LANES), 0)
-    lane2 = iota((8, LANES), 1)
+        eddies.append(pick(sign * strength))
+    eddy_row = jnp.broadcast_to(jnp.concatenate(eddies[:4], axis=1), (8, LANES))
+    eddy_rest = jnp.broadcast_to(jnp.concatenate([eddies[4]] * 4, axis=1), (8, LANES))
     for k in range(4):
-        tile_a = regrouped(partial[:4], k)
-        tile_b = regrouped([partial[4], extra, edge, faces], k)
-        for x in range(8):
-            send[pl.ds(k * 128 + x, 8, stride=16), :] = tile_a[x]
-            tile = tile_b[x]
-            if 1 <= x <= 5:
-                tile = jnp.where(lane2 // 32 == 1, eddies[x : x + 1, :], tile)
-            elif x == 6:
-                tile = jnp.where(lane2 // 32 == 1, 0.0, tile)
-            send[pl.ds(k * 128 + 8 + x, 8, stride=16), :] = tile
+        cells = regrouped(partial[:4], k)
+        rows = [cells[x] for x in range(8)]
+        rows += [regrouped([partial[4][4 * a + b] for b in range(4)], k) for a in range(2)]
+        rows += [regrouped([flux_x[f][x] for f in range(4)], k) for x in (7, 0)]
+        rows += [regrouped(sides, k), eddy_row]
+        ends = [jnp.zeros_like(eddy_rest), flux_x[4][7], flux_x[4][0], jnp.zeros_like(eddy_rest)]
+        rows.append(jnp.where(lane2 < 32, eddy_rest, regrouped(ends, k)))
+        for r, value in enumerate(rows):
+            send[pl.ds(8 * SENT * k + r, 8, stride=SENT), :] = value
 
 
 def dot_nt(a, b):
@@ -412,8 +406,11 @@
     lane = iota((8, 8, LANES), 2) % 32
     halo = edge[...]
 
+    shift = jnp.where(first_core, 31, LANES)
+    sign = jnp.where(first_core, 1.0, -1.0)
+
     def y_whole(a, i):
-        near = jnp.where(first_core, roll(halo, 31 - i, 2), -roll(halo, -i, 2))
+        near = jnp.stack([pltpu.roll(halo[i], shift - x, 1) for x in range(8)]) * sign
         near = jnp.where(lane == jnp.where(first_core, 31, 0), near, 0.0)
         return y_difference(a, first_core) + near
 
@@ -432,8 +429,11 @@
     weight = sensor * mask[None]
     for k in range(4):
         updated_out[k] = regrouped(updated[:4], k)
-        energy_out[k] = roll(updated[4], -32 * k, 2)
         weight_out[k] = regrouped([weight] * 4, k)
+        for a in range(2):
+            four = range(4 * a, 4 * a + 4)
+            energy_out[0, k, a] = regrouped([updated[4][x] for x in four], k)
+            energy_out[1, k, a] = regrouped([weight[x] for x in four], k)
     for i, a in enumerate(updated + rates):
         ends_out[i, 0] = a[0]
         ends_out[i, 1] = a[7]
@@ -446,7 +446,12 @@
     for end in range(2):
         bins_out[0, end] = dil[7 * end]
         bins_out[1, end] = vort[7 * end]
-    matrix_out[0], matrix_out[1] = halves(matrix[...])
+    rows = jnp.concatenate([matrix[pl.ds(r, 16, stride=8), :] for r in range(8)], axis=0)
+    source, target = iota((LANES, LANES), 0), iota((LANES, LANES), 1)
+    order = jnp.where(source == 8 * (target % 16) + target // 16, 1.0, 0.0).astype(jnp.bfloat16)
+    for i, part in enumerate(halves(rows)):
+        ordered = jnp.dot(part, order, preferred_element_type=jnp.float32)
+        matrix_out[i] = ordered.astype(jnp.bfloat16)
     mask_out[...] = jnp.broadcast_to(mask, (8, LANES))
 
 
@@ -474,26 +479,29 @@
     lane = iota((8, LANES), 1)
     peak = HAT_PEAK * HAT_PEAK
 
-    chunk_tile = lambda g, h, t: received[pl.ds(32 * g + 16 * h + 8 * t, 8), :]
-    tiles = [[chunk_tile(g, h, 1) for g in range(16)] for h in range(2)]
-    chunks = []
-    for h in range(2):
-        for a in range(4):
-            out = None
-            for i in range(4):
-                moved = roll(tiles[h][4 * a + i], 32 * (i - 1), 1)
-                out = moved if out is None else jnp.where(lane // 32 == i, moved, out)
-            chunks.append(out)
+    def side_by_side(r, group):
+        out = None
+        for j in range(4):
+            moved = received[pl.ds(SENT * j + r, 8, stride=4 * SENT), :]
+            moved = roll(moved, 32 * (j - group), 1)
+            out = moved if out is None else jnp.where(lane // 32 == j, moved, out)
+        return out
+
+    centre_y, centre_z = side_by_side(13, 0), side_by_side(13, 1)
+    strength = [side_by_side(13, 2), side_by_side(13, 3), side_by_side(14, 0)]
+    strength = [a * peak for a in strength]
+    hat = span_hat(plane, centre_z, 32.0)
     y_all = iota((64, LANES), 0).astype(jnp.float32)
     lhs, rhs = [], []
-    for chunk in chunks:
-        weighted = (chunk * peak) * span_hat(plane, chunk[2:3], 32.0)
-        lhs.append(jnp.where((row >= 3) & (row <= 5), weighted, 0.0))
-        rhs.append(normal_hat(y_all, chunk[1:2]))
+    for c in range(8):
+        weighted = jnp.where(row == 1, strength[1][c : c + 1], strength[2][c : c + 1])
+        weighted = jnp.where(row == 0, strength[0][c : c + 1], weighted)
+        lhs.append(jnp.where(row < 3, weighted * hat[c : c + 1], 0.0))
+        rhs.append(normal_hat(y_all, centre_y[c : c + 1]))
     high, low = halves(jnp.concatenate(lhs, axis=1))
     inflow = dot_nt(jnp.concatenate([high, low], axis=0), jnp.concatenate(rhs, axis=1))
     inflow = inflow[:8] + inflow[8:]
-    ghost = ghost_state_rows(inflow[3:4], inflow[4:5], inflow[5:6])
+    ghost = ghost_state_rows(inflow[0:1], inflow[1:2], inflow[2:3])
     ghost_vel, ghost_pressure = velocity_pressure(ghost)
     ghost_x = euler_flux(ghost, ghost_vel, ghost_pressure, 0)
 
@@ -502,10 +510,10 @@
         z_all = iota((32, LANES), 0).astype(jnp.float32)
         y_own = (iota((32, LANES), 0) + core * 32).astype(jnp.float32)
         lhs, rhs = [], []
-        for chunk in chunks:
-            hat = span_hat(z_all, chunk[2:3], 32.0) * peak
-            lhs.append(jnp.concatenate([hat * chunk[3 + c : 4 + c] for c in range(3)], axis=0))
-            rhs.append(normal_hat(y_own, chunk[1:2]))
+        for c in range(8):
+            hat = span_hat(z_all, centre_z[c : c + 1], 32.0)
+            lhs.append(jnp.concatenate([hat * a[c : c + 1] for a in strength], axis=0))
+            rhs.append(normal_hat(y_own, centre_y[c : c + 1]))
         high, low = halves(jnp.concatenate(lhs, axis=1))
         own = dot_nt(jnp.concatenate([high, low], axis=0), jnp.concatenate(rhs, axis=1))
         own = own[:96] + own[96:]
@@ -521,47 +529,38 @@
     def _():
         before[...] = jnp.where(odd, pair[...], far[...])
 
-    chunk_row = lambda r: received[pl.ds(8 + r, 32, stride=16), :]
-    group = iota((32, LANES), 1) // 32
-    faces = []
-    for slots in ((0, 2, 4, 6), (7, 1, 3, 5)):
-        side = None
-        for f, r in enumerate(slots):
-            moved = roll(chunk_row(r), 32 * (f - 3), 1)
-            side = moved if side is None else jnp.where(group == f, moved, side)
-        faces.append((side, roll(chunk_row(slots[0]), -32, 1)))
-    last_faces, first_faces = faces
-    columns_a, columns_e = [], []
+    row16 = iota((16, LANES), 0)
+    lane16 = iota((16, LANES), 1)
+    chunk_row = lambda r, h: received[pl.ds(SENT * h + r, 16, stride=2 * SENT), :]
+    columns, energy_columns = [], []
     for h in range(2):
         own = slice(32 * h, 32 * h + 32)
+        target = 31 if h == 0 else 0
+        side = -HALF_STEP if h == 0 else HALF_STEP
+        across = side * chunk_row(12, 1 - h)
         ghost_a = jnp.concatenate([ghost_x[f][:, own] for f in range(4)], axis=1)
         ghost_e = jnp.concatenate([ghost_x[4][:, own]] * 4, axis=1)
-        ca, ce = [], []
-        for g in range(16):
-            zero = jnp.zeros((1, LANES), jnp.float32)
-            i, j = 2 * g + h - 2, 2 * g + h + 2
-            previous_a, previous_e = ghost_a, ghost_e
-            if g > 0:
-                previous_a, previous_e = last_faces[0][i : i + 1], last_faces[1][i : i + 1]
-            next_a, next_e = zero, zero
-            if g < 15:
-                next_a, next_e = first_faces[0][j : j + 1], first_faces[1][j : j + 1]
-            fix_a = jnp.where(row == 0, previous_a, jnp.where(row == 7, -next_a, 0.0))
-            fix_e = jnp.where(row == 0, previous_e, jnp.where(row == 7, -next_e, 0.0))
-            other = tiles[1 - h][g]
-            target = 31 if h == 0 else 0
-            side = -1.0 if h == 0 else 1.0
-            for f in range(4):
-                moved = roll(other, 32 * f + target - (64 + f), 1)
-                fix_a = jnp.where(lane == 32 * f + target, fix_a + side * moved, fix_a)
-            moved = roll(other, target - 68, 1)
-            fix_e = jnp.where(lane == target, fix_e + side * moved, fix_e)
-            ca.append(chunk_tile(g, h, 0) + HALF_STEP * fix_a)
-            ce.append(jnp.where(lane < 32, tiles[h][g] + HALF_STEP * fix_e, 0.0))
-        columns_a.append(jnp.concatenate(ca, axis=0))
-        columns_e.append(jnp.concatenate(ce, axis=0))
+        both_ends = chunk_row(14, h)
+        last_a, first_a = chunk_row(10, h), chunk_row(11, h)
+        last_e, first_e = roll(both_ends, -32, 1), roll(both_ends, -64, 1)
+        before_a = jnp.where(row16 == 0, ghost_a, roll(last_a, 1, 0))
+        before_e = jnp.where(row16 == 0, ghost_e, roll(last_e, 1, 0))
+        after_a = jnp.where(row16 == 15, 0.0, roll(first_a, -1, 0))
+        after_e = jnp.where(row16 == 15, 0.0, roll(first_e, -1, 0))
+        for r in range(8):
+            a = chunk_row(r, h)
+            e = roll(chunk_row(8 + r // 4, h), -32 * (r % 4), 1)
+            if r == 0:
+                a, e = a + HALF_STEP * before_a, e + HALF_STEP * before_e
+            if r == 7:
+                a, e = a - HALF_STEP * after_a, e - HALF_STEP * after_e
+            a = jnp.where(lane16 % 32 == target, a + roll(across, target - r, 1), a)
+            e = jnp.where(lane16 == target, e + roll(across, target - r - 8, 1), e)
+            columns.append(a)
+            energy_columns.append(roll(e, 32 * h, 1))
+    joined = [jnp.where(lane16 < 32, energy_columns[r], energy_columns[8 + r]) for r in range(8)]
     columns = jnp.concatenate(
-        [columns_a[0], columns_a[1], columns_e[0] + roll(columns_e[1], 32, 1)], axis=1
+        [jnp.concatenate(part, axis=0) for part in (columns[:8], columns[8:], joined)], axis=1
     )
     m_high, m_low = matrix[0], matrix[1]
     c_high, c_low = halves(columns)
@@ -587,20 +586,27 @@
         weight = sensor * mask[...]
         for k in range(4):
             updated_out[end, k] = regrouped(updated[:4], k)
-            energy_out[end, k] = roll(updated[4], -32 * k, 1)
+            energy_out[end, k] = roll(updated[4], 32 * (3 * end - k), 1)
             weight_out[end, k] = regrouped([weight] * 4, k)
         sensors.append(sensor)
         dils.append(bins[0, end])
         vorts.append(bins[1, end])
     counts = counts_in[...] + counted(sensors, dils, vorts)
-    counts = jnp.concatenate([jnp.zeros((8, 64), jnp.float32), counts], axis=1)
-
-    for g in range(16):
-        block = smooth[8 * g : 8 * g + 8]
-        for h in range(2):
-            send[g, h, 0] = block[:, 128 * h : 128 * h + 128]
-            own_energy = roll(block[:, 256:], -32 * h, 1)
-            send[g, h, 1] = jnp.where(lane < 32, own_energy, counts)
+
+    for h in range(2):
+        back_row = lambda r: (pl.ds(BACK * h + r, 16, stride=2 * BACK), slice(None))
+        for r in range(8):
+            send[back_row(r)] = smooth[16 * r : 16 * r + 16, 128 * h : 128 * h + 128]
+        for a in range(2):
+            out = None
+            for b in range(4):
+                r = 4 * a + b
+                moved = roll(smooth[16 * r : 16 * r + 16, 256:], 32 * (b - h), 1)
+                out = moved if out is None else jnp.where(lane16 // 32 == b, moved, out)
+            send[back_row(8 + a)] = out
+        for i in range(3):
+            pair_of_bins = jnp.concatenate([counts[2 * i : 2 * i + 1], counts[2 * i + 1 : 2 * i + 2]], axis=1)
+            send[back_row(10 + i)] = jnp.broadcast_to(pair_of_bins, (16, LANES))
 
 
 def final_kernel(
@@ -616,27 +622,34 @@
     histogram,
     totals,
 ):
+    group = iota((8, LANES), 1) // 32
     for k in range(4):
+        planes = pl.ds(8 * k, 8)
+        chunk_row = lambda r: received[pl.ds(8 * BACK * k + r, 8, stride=BACK), :]
         for x in range(8):
             if x in (0, 7):
-                end = x // 7
-                u, e, w = end_updated[end, k], end_energy[end, k], end_weight[end, k]
+                u, w = end_updated[x // 7, k], end_weight[x // 7, k]
             else:
-                u, e, w = updated[k, x], energy[k, x], weight[k, x]
-            smooth = received[pl.ds(k * 128 + x, 8, stride=16), :]
-            result = u + w * (smooth - u)
+                u, w = updated[k, x], weight[k, x]
+            result = u + w * (chunk_row(x) - u)
             for f in range(4):
-                conserved[f, x, 8 * k : 8 * k + 8, :] = result[:, 32 * f : 32 * f + 32]
-            smooth = received[pl.ds(k * 128 + 8 + x, 8, stride=16), :]
-            result = e + w * (smooth - e)
-            conserved[4, x, 8 * k : 8 * k + 8, :] = result[:, :32]
-    totals[...] = jnp.zeros_like(totals)
-    for g in range(16):
-        both = received[32 * g + 8 : 32 * g + 16, :] + received[32 * g + 24 : 32 * g + 32, :]
-        totals[4 * g : 4 * g + 8, :] = totals[4 * g : 4 * g + 8, :] + both
-    first = totals[0:8, :] + totals[64:72, :]
-    table = jnp.concatenate([first, totals[8:64, :]], axis=0)[:, 64:]
-    histogram[...] = table.T * scale
+                conserved[f, x, planes, :] = result[:, 32 * f : 32 * f + 32]
+        for a in range(2):
+            ours = group == 3 * a
+            u = jnp.where(ours, end_energy[a, k], energy[0, k, a])
+            w = jnp.where(ours, end_weight[a, k], energy[1, k, a])
+            result = u + w * (chunk_row(8 + a) - u)
+            for b in range(4):
+                conserved[4, 4 * a + b, planes, :] = result[:, 32 * b : 32 * b + 32]
+
+    bins = []
+    for i in range(3):
+        both = [received[pl.ds(BACK * h + 10 + i, 16, stride=2 * BACK), :] for h in range(2)]
+        bins.append(both[0] + both[1])
+    first = bins[0] + roll(bins[2], 1, 0)
+    for c, part in enumerate((first, roll(bins[0], 64, 1), bins[1], roll(bins[1], 64, 1))):
+        totals[pl.ds(c, 16, stride=4), :] = part
+    histogram[...] = totals[:, :64].T * scale
 
 
 def shards(
@@ -679,7 +692,7 @@
     near = lambda a: pltpu.with_memory_space_constraint(a, pltpu.VMEM)
     send, far, pair, edge = pl.pallas_call(
         lambda *refs: slab_kernel(amplitude, *refs),
-        out_shape=[vmem(512, LANES), vmem(5, 8, LANES), vmem(5, 8, LANES), vmem(*cells)],
+        out_shape=[vmem(32 * SENT, LANES), vmem(5, 8, LANES), vmem(5, 8, LANES), vmem(*cells)],
         name="slab",
     )(
         density,
@@ -690,7 +703,7 @@
         eddy_signs.T,
         eddy_strengths.reshape(1, -1),
     )
-    received = lax.all_to_all(send.reshape(32, 16, LANES), ("gx", "gy"), 0, 0, tiled=True)
+    received = lax.all_to_all(send.reshape(32, SENT, 1, LANES), ("gx", "gy"), 0, 0, tiled=True)
     both = lambda first: [p for i in range(first, slabs - 1, 2) for p in ((i, i + 1), (i + 1, i))]
     far = lax.ppermute(far, "gx", both(1))
     pair = lax.ppermute(pair, "gx", both(0))
@@ -699,7 +712,7 @@
         interior_kernel,
         out_shape=[
             vmem(4, *cells),
-            vmem(4, *cells),
+            vmem(2, 4, 2, 8, LANES),
             vmem(4, *cells),
             vmem(9, 2, 8, LANES),
             vmem(8, 64),
@@ -721,21 +734,24 @@
     )
     send, *end_rows = pl.pallas_call(
         pencil_kernel,
-        out_shape=[vmem(16, 2, 2, 8, LANES)] + [vmem(2, 4, 8, LANES)] * 3,
+        out_shape=[vmem(32 * BACK, LANES)] + [vmem(2, 4, 8, LANES)] * 3,
         scratch_shapes=[pltpu.VMEM((5, 8, LANES), jnp.float32)],
         name="pencil",
     )(
-        near(received.reshape(512, LANES)),
+        near(received.reshape(32 * SENT, LANES)),
         *map(near, (matrix, ends, counts, bins, mask, far, pair)),
     )
-    received = lax.all_to_all(send.reshape(32, 16, LANES), ("gx", "gy"), 0, 0, tiled=True)
+    received = lax.all_to_all(send.reshape(32, BACK, 1, LANES), ("gx", "gy"), 0, 0, tiled=True)
     scale = HISTOGRAM_BINS * HISTOGRAM_BINS / (cells_x * slabs * span * total_y)
     conserved_next, histogram = pl.pallas_call(
         lambda *refs: final_kernel(scale, *refs),
         out_shape=[f32(5, cells_x, span, cells_y), f32(HISTOGRAM_BINS, HISTOGRAM_BINS)],
-        scratch_shapes=[pltpu.VMEM((72, LANES), jnp.float32)],
+        scratch_shapes=[vmem(HISTOGRAM_BINS, LANES)],
         name="final",
-    )(*map(near, (received.reshape(512, LANES), updated, updated_energy, weight, *end_rows)))
+    )(
+        near(received.reshape(32 * BACK, LANES)),
+        *map(near, (updated, updated_energy, weight, *end_rows)),
+    )
     return (conserved_next, histogram)
 
 

time: 36.5 us -> 34.6 us (0.948)
  blocking collectives: 12.6 us -> 11.3 us
    all_to_all x1, blocking collectives: 12.6 us -> 11.3 us  [shards(): lax.all_to_all(send.reshape(32, BACK, 1, LANES), ('gx', 'gy'), 0, 0, tile...]
where the time goes in v4:
time: 34.6 us; the launch traced here: 34.4 us
  starting transfers between devices  12.7 us (37%)
  blocking collectives  11.3 us (33%)
  Pallas kernels  6.87 us (20%)
  waiting for transfers between devices  2.75 us (8%)
  between operations  0.68 us (2%)
    all_to_all x1, blocking collectives, shards(): lax.all_to_all(send.reshape(32, BACK, 1, LANES), ('gx', 'gy'), 0, 0, tile...  11.3 us
    all_to_all x1, starting transfers between devices, shards(): lax.all_to_all(send.reshape(32, SENT, 1, LANES), ('gx', 'gy'), 0, 0, tile...  7.3 us
    ppermute x1, starting transfers between devices, shards(): pair = lax.ppermute(pair, 'gx', both(0))  4.45 us
    all_to_all x1, waiting for transfers between devices, shards(): lax.all_to_all(send.reshape(32, SENT, 1, LANES), ('gx', 'gy'), 0, 0, tile...  2.74 us
    pallas_call x1, Pallas kernels, shards(): pl.pallas_call(lambda *refs: slab_kernel(amplitude, *refs), out_shape=[vm...  2.56 us
    pallas_call x1, Pallas kernels, shards(): pl.pallas_call(interior_kernel, out_shape=[vmem(4, *cells), vmem(2, 4, 2,...  2.09 us
    pallas_call x1, Pallas kernels, shards(): pl.pallas_call(pencil_kernel, out_shape=[vmem(32 * BACK, LANES)] + [vmem(...  1.17 us
    pallas_call x1, Pallas kernels, shards(): pl.pallas_call(lambda *refs: final_kernel(scale, *refs), out_shape=[f32(5...  1.05 us
  transfers between devices with their start and end apart: 4, of which 1 were waited for; matrix products, arithmetic and copies ran while one was open for 0% of the time, Pallas kernels for 6%

profile of v4, /device:TPU:0, one launch (start us, length us, event | category | flops | bytes accessed | tf_op | source)
XLA Modules:
  0.0 34.4 jit_solution(12528949800321074263)
XLA Ops:
  0.6 2.6 %slab.1 = (f32[480,128]{1,0:T(8,128)}, f32[5,8,128]{2,1,0:T(8,128)S(1)}, f32[5,8,128]{2,1,0:T(8,128)S(1)}, f32[8,8,128]{2,1,0:T(8,128)S(1)}) custom-call(f32[8,32,32]{2,1,0:T(8,128)} %density.1, f32[3,8,32,32]{3,2,1,0:T(8,128)} %momentum.1, f32[8,32,32]{2,1,0:T(8,128)} %energy.1, s32[1,64]{1,0:T(1,128)} %bitcast.14, s32[1,64]{1,0:T(1,128)} %bitcast.15, ...), custom_call_target="tpu_custom_call" | custom-call | tf_op jit(solution)/shard_map/slab/pallas_call | solution.py:693
  3.2 7.3 %all-to-all-start = ((f32[32,15,1,128]{3,2,1,0:T(1,128)}), f32[32,15,1,128]{3,2,1,0:T(1,128)S(1)}, u32[]{:S(2)}, u32[]{:S(2)}) async-start(f32[32,15,1,128]{3,2,1,0:T(1,128)} %bitcast.4), calls=%async_computation | async-start | bytes 491520 | tf_op jit(solution)/shard_map/all_to_all | solution.py:706
  10.5 0.3 collective-permute-start
  10.8 0.7 %collective-permute-start.1 = (f32[5,8,128]{2,1,0:T(8,128)S(1)}, f32[5,8,128]{2,1,0:T(8,128)S(1)}, u32[]{:S(2)}, u32[]{:S(2)}) collective-permute-start(f32[5,8,128]{2,1,0:T(8,128)S(1)} %get-tuple-element.25), channel_id=1, source_target_pairs={{2,4},{4,2},{6,8},{8,6},{10,12},{12,10},{14,16},{16,14},{18,20},{2... | collective-permute-start | bytes 61448 | tf_op jit(solution)/shard_map/ppermute | solution.py:708
  11.5 4.5 %collective-permute-start.2 = (f32[5,8,128]{2,1,0:T(8,128)S(1)}, f32[5,8,128]{2,1,0:T(8,128)S(1)}, u32[]{:S(2)}, u32[]{:S(2)}) collective-permute-start(f32[5,8,128]{2,1,0:T(8,128)S(1)} %get-tuple-element.26), channel_id=1, source_target_pairs={{0,2},{2,0},{4,6},{6,4},{8,10},{10,8},{12,14},{14,12},{16,18},{18,... | collective-permute-start | bytes 61448 | tf_op jit(solution)/shard_map/ppermute | solution.py:709
  15.9 0.0 collective-permute-done.edge
  15.9 2.1 %interior.1 = (f32[4,8,8,128]{3,2,1,0:T(8,128)S(1)}, f32[2,4,2,8,128]{4,3,2,1,0:T(8,128)S(1)}, f32[4,8,8,128]{3,2,1,0:T(8,128)S(1)}, f32[9,2,8,128]{3,2,1,0:T(8,...) custom-call(f32[8,32,32]{2,1,0:T(8,128)} %density.1, ...), custom_call_target="tpu_custom_call" | custom-call | flops 10000000 | bytes 2000000 | tf_op jit(solution)/shard_map/interior/pallas_call | solution.py:711
  18.0 0.0 collective-permute-done.1.far
  18.0 0.0 collective-permute-done.2.pair
  18.0 2.7 %all-to-all-done = f32[32,15,1,128]{3,2,1,0:T(1,128)S(1)} async-done(((f32[32,15,1,128]{3,2,1,0:T(1,128)}), f32[32,15,1,128]{3,2,1,0:T(1,128)S(1)}, u32[]{:S(2)}, u32[]{:S(2)}) %all-to-all-start) | async-done | bytes 245792 | tf_op jit(solution)/shard_map/all_to_all | solution.py:706
  20.8 1.2 %pencil.1 = (f32[416,128]{1,0:T(8,128)S(1)}, f32[2,4,8,128]{3,2,1,0:T(8,128)S(1)}, f32[2,4,8,128]{3,2,1,0:T(8,128)S(1)}, f32[2,4,8,128]{3,2,1,0:T(8,128)S(1)}) custom-call(f32[480,128]{1,0:T(8,128)S(1)} %bitcast.9, bf16[2,128,128]{2,1,0:T(8,128)(2,1)S(1)} %get-tuple-element.20.matrix, f32[9,2,8,128]{3,2,1,0:T(8,128)S(1)} %get-tuple-element.21.ends, ...), custom_call_target="tpu_custom_call" | custom-call | tf_op jit(solution)/shard_map/pencil/pallas_call | solution.py:735
  22.0 11.3 %all_to_all.10 = f32[32,13,1,128]{3,2,1,0:T(1,128)S(1)} all-to-all(f32[32,13,1,128]{3,2,1,0:T(1,128)S(1)} %bitcast.11), channel_id=1, replica_groups=mesh['gx'=16,'gy'=2] {'gx','gy'}, dimensions={0} | all-to-all | bytes 425984 | tf_op jit(solution)/shard_map/all_to_all | solution.py:744
  33.3 1.0 %final.1 = (f32[5,8,32,32]{3,2,1,0:T(8,128)}, f32[64,64]{1,0:T(8,128)}) custom-call(f32[416,128]{1,0:T(8,128)S(1)} %bitcast.10, f32[4,8,8,128]{3,2,1,0:T(8,128)S(1)} %get-tuple-element.28.refs_1_, f32[2,4,2,8,128]{4,3,2,1,0:T(8,128)S(1)} %get-tuple-element.29.refs_2_, f32[4,8,8,128]{3,2,1,0:T(8,128)S(1)} %get-tuple-element.30.refs_3_, ...), custom_call_target="tpu_custom_call" | custom-call | tf_op jit(solution)/shard_map/final/pallas_call | solution.py:746
Async XLA Ops:
  3.2 17.6 %all-to-all-start = ((f32[32,15,1,128]{3,2,1,0:T(1,128)}), f32[32,15,1,128]{3,2,1,0:T(1,128)S(1)}, u32[]{:S(2)}, u32[]{:S(2)}) async-start(f32[32,15,1,128]{3,2,1,0:T(1,128)} %bitcast.4), calls=%async_computation | async-start | bytes 491520 | tf_op jit(solution)/shard_map/all_to_all | solution.py:706
  10.5 5.4 %collective-permute-start = (f32[8,8,128]{2,1,0:T(8,128)S(1)}, f32[8,8,128]{2,1,0:T(8,128)S(1)}, u32[]{:S(2)}, u32[]{:S(2)}) collective-permute-start(f32[8,8,128]{2,1,0:T(8,128)S(1)} %get-tuple-element.19), channel_id=1, source_target_pairs={{0,1},{1,0},{2,3},{3,2},{4,5},{5,4},{6,7},{7,6},{8,9},{9,8},{10,11... | collective-permute-start | bytes 98312 | tf_op jit(solution)/shard_map/ppermute | solution.py:710
  10.8 7.2 %collective-permute-start.1 = (f32[5,8,128]{2,1,0:T(8,128)S(1)}, f32[5,8,128]{2,1,0:T(8,128)S(1)}, u32[]{:S(2)}, u32[]{:S(2)}) collective-permute-start(f32[5,8,128]{2,1,0:T(8,128)S(1)} %get-tuple-element.25), channel_id=1, source_target_pairs={{2,4},{4,2},{6,8},{8,6},{10,12},{12,10},{14,16},{16,14},{18,20},{2... | collective-permute-start | bytes 61448 | tf_op jit(solution)/shard_map/ppermute | solution.py:708
  11.5 6.6 %collective-permute-start.2 = (f32[5,8,128]{2,1,0:T(8,128)S(1)}, f32[5,8,128]{2,1,0:T(8,128)S(1)}, u32[]{:S(2)}, u32[]{:S(2)}) collective-permute-start(f32[5,8,128]{2,1,0:T(8,128)S(1)} %get-tuple-element.26), channel_id=1, source_target_pairs={{0,2},{2,0},{4,6},{6,4},{8,10},{10,8},{12,14},{14,12},{16,18},{18,... | collective-permute-start | bytes 61448 | tf_op jit(solution)/shard_map/ppermute | solution.py:709

commit v5 on v4

--- a/solution.py
+++ b/solution.py
@@ -216,13 +216,21 @@
     return jnp.concatenate(parts, axis=-1)
 
 
-def regrouped(parts, k):
-    group = iota(parts[0].shape, len(parts[0].shape) - 1) // 32
-    out = None
-    for i, part in enumerate(parts):
-        moved = roll(part, 32 * (i - k), len(part.shape) - 1)
-        out = moved if out is None else jnp.where(group == i, moved, out)
+def regrouped(parts):
+    axis = len(parts[0].shape) - 1
+    group = iota(parts[0].shape, axis) // 32
+    turned = [roll(part, 32 * i, axis) for i, part in enumerate(parts)]
+    out = []
+    for k in range(4):
+        mixed = turned[0]
+        for i in range(1, 4):
+            mixed = jnp.where(group == (k + i) % 4, turned[i], mixed)
+        out.append(roll(mixed, -32 * k, axis))
     return out
+
+
+def repeated(part):
+    return regrouped([part] * 4)
 
 
 def velocity_pressure(q):
@@ -314,14 +322,14 @@
         eddies.append(pick(sign * strength))
     eddy_row = jnp.broadcast_to(jnp.concatenate(eddies[:4], axis=1), (8, LANES))
     eddy_rest = jnp.broadcast_to(jnp.concatenate([eddies[4]] * 4, axis=1), (8, LANES))
+    cells = regrouped(partial[:4])
+    energies = [regrouped([partial[4][4 * a + b] for b in range(4)]) for a in range(2)]
+    faces = [regrouped([flux_x[f][x] for f in range(4)]) for x in (7, 0)]
+    blank = jnp.zeros_like(eddy_rest)
+    sides, ends = regrouped(sides), regrouped([blank, flux_x[4][7], flux_x[4][0], blank])
     for k in range(4):
-        cells = regrouped(partial[:4], k)
-        rows = [cells[x] for x in range(8)]
-        rows += [regrouped([partial[4][4 * a + b] for b in range(4)], k) for a in range(2)]
-        rows += [regrouped([flux_x[f][x] for f in range(4)], k) for x in (7, 0)]
-        rows += [regrouped(sides, k), eddy_row]
-        ends = [jnp.zeros_like(eddy_rest), flux_x[4][7], flux_x[4][0], jnp.zeros_like(eddy_rest)]
-        rows.append(jnp.where(lane2 < 32, eddy_rest, regrouped(ends, k)))
+        rows = [cells[k][x] for x in range(8)] + [e[k] for e in energies] + [a[k] for a in faces]
+        rows += [sides[k], eddy_row, jnp.where(lane2 < 32, eddy_rest, ends[k])]
         for r, value in enumerate(rows):
             send[pl.ds(8 * SENT * k + r, 8, stride=SENT), :] = value
 
@@ -427,13 +435,16 @@
     sensor = sensor_of(*rates)
     mask = jnp.concatenate([switch[...].astype(jnp.float32)] * 4, axis=1)
     weight = sensor * mask[None]
+    cells, weights = regrouped(updated[:4]), repeated(weight)
     for k in range(4):
-        updated_out[k] = regrouped(updated[:4], k)
-        weight_out[k] = regrouped([weight] * 4, k)
-        for a in range(2):
-            four = range(4 * a, 4 * a + 4)
-            energy_out[0, k, a] = regrouped([updated[4][x] for x in four], k)
-            energy_out[1, k, a] = regrouped([weight[x] for x in four], k)
+        updated_out[k] = cells[k]
+        weight_out[k] = weights[k]
+    for a in range(2):
+        energies = regrouped([updated[4][x] for x in range(4 * a, 4 * a + 4)])
+        weights = regrouped([weight[x] for x in range(4 * a, 4 * a + 4)])
+        for k in range(4):
+            energy_out[0, k, a] = energies[k]
+            energy_out[1, k, a] = weights[k]
     for i, a in enumerate(updated + rates):
         ends_out[i, 0] = a[0]
         ends_out[i, 1] = a[7]
@@ -490,21 +501,6 @@
     centre_y, centre_z = side_by_side(13, 0), side_by_side(13, 1)
     strength = [side_by_side(13, 2), side_by_side(13, 3), side_by_side(14, 0)]
     strength = [a * peak for a in strength]
-    hat = span_hat(plane, centre_z, 32.0)
-    y_all = iota((64, LANES), 0).astype(jnp.float32)
-    lhs, rhs = [], []
-    for c in range(8):
-        weighted = jnp.where(row == 1, strength[1][c : c + 1], strength[2][c : c + 1])
-        weighted = jnp.where(row == 0, strength[0][c : c + 1], weighted)
-        lhs.append(jnp.where(row < 3, weighted * hat[c : c + 1], 0.0))
-        rhs.append(normal_hat(y_all, centre_y[c : c + 1]))
-    high, low = halves(jnp.concatenate(lhs, axis=1))
-    inflow = dot_nt(jnp.concatenate([high, low], axis=0), jnp.concatenate(rhs, axis=1))
-    inflow = inflow[:8] + inflow[8:]
-    ghost = ghost_state_rows(inflow[0:1], inflow[1:2], inflow[2:3])
-    ghost_vel, ghost_pressure = velocity_pressure(ghost)
-    ghost_x = euler_flux(ghost, ghost_vel, ghost_pressure, 0)
-
     @pl.when(slab == 0)
     def _():
         z_all = iota((32, LANES), 0).astype(jnp.float32)
@@ -529,22 +525,34 @@
     def _():
         before[...] = jnp.where(odd, pair[...], far[...])
 
+    hat = span_hat(plane, centre_z, 32.0)
+    y_all = iota((64, LANES), 0).astype(jnp.float32)
+    lhs, rhs = [], []
+    for c in range(8):
+        weighted = jnp.where(row == 1, strength[1][c : c + 1], strength[2][c : c + 1])
+        weighted = jnp.where(row == 0, strength[0][c : c + 1], weighted)
+        lhs.append(jnp.where(row < 3, weighted * hat[c : c + 1], 0.0))
+        rhs.append(normal_hat(y_all, centre_y[c : c + 1]))
+    high, low = halves(jnp.concatenate(lhs, axis=1))
+    inflow = dot_nt(jnp.concatenate([high, low], axis=0), jnp.concatenate(rhs, axis=1))
+    inflow = inflow[:8] + inflow[8:]
+    ghost = ghost_state_rows(inflow[0:1], inflow[1:2], inflow[2:3])
+    ghost_vel, ghost_pressure = velocity_pressure(ghost)
+    ghost_x = euler_flux(ghost, ghost_vel, ghost_pressure, 0)
+
     row16 = iota((16, LANES), 0)
     lane16 = iota((16, LANES), 1)
     chunk_row = lambda r, h: received[pl.ds(SENT * h + r, 16, stride=2 * SENT), :]
     columns, energy_columns = [], []
     for h in range(2):
-        own = slice(32 * h, 32 * h + 32)
         target = 31 if h == 0 else 0
         side = -HALF_STEP if h == 0 else HALF_STEP
         across = side * chunk_row(12, 1 - h)
-        ghost_a = jnp.concatenate([ghost_x[f][:, own] for f in range(4)], axis=1)
-        ghost_e = jnp.concatenate([ghost_x[4][:, own]] * 4, axis=1)
         both_ends = chunk_row(14, h)
         last_a, first_a = chunk_row(10, h), chunk_row(11, h)
         last_e, first_e = roll(both_ends, -32, 1), roll(both_ends, -64, 1)
-        before_a = jnp.where(row16 == 0, ghost_a, roll(last_a, 1, 0))
-        before_e = jnp.where(row16 == 0, ghost_e, roll(last_e, 1, 0))
+        before_a = jnp.where(row16 == 0, 0.0, roll(last_a, 1, 0))
+        before_e = jnp.where(row16 == 0, 0.0, roll(last_e, 1, 0))
         after_a = jnp.where(row16 == 15, 0.0, roll(first_a, -1, 0))
         after_e = jnp.where(row16 == 15, 0.0, roll(first_e, -1, 0))
         for r in range(8):
@@ -570,6 +578,11 @@
         + jnp.dot(m_low, c_high, preferred_element_type=jnp.float32)
     )
 
+    first_column = (m_high[:, :1].astype(jnp.float32) + m_low[:, :1].astype(jnp.float32)) * HALF_STEP
+    inflow_flux = [ghost_x[f][:, 32 * h : 32 * h + 32] for h in range(2) for f in range(4)]
+    inflow_flux += [ghost_x[4], jnp.zeros((1, 64), jnp.float32)]
+    smooth = smooth + first_column * jnp.concatenate(inflow_flux, axis=1)
+
     sensors, dils, vorts = [], [], []
     for end in range(2):
         q = [jnp.where(odd, far[f], pair[f]) if end else before[f] for f in range(5)]
@@ -584,10 +597,11 @@
         rates = [rates[0] + add[5], rates[1], rates[2] - add[7], rates[3] + add[6]]
         sensor = sensor_of(*rates)
         weight = sensor * mask[...]
+        cells, weights = regrouped(updated[:4]), repeated(weight)
         for k in range(4):
-            updated_out[end, k] = regrouped(updated[:4], k)
+            updated_out[end, k] = cells[k]
             energy_out[end, k] = roll(updated[4], 32 * (3 * end - k), 1)
-            weight_out[end, k] = regrouped([weight] * 4, k)
+            weight_out[end, k] = weights[k]
         sensors.append(sensor)
         dils.append(bins[0, end])
         vorts.append(bins[1, end])

time: 34.6 us -> 34.4 us (level)
  no operation moved by 1% of the time
where the time goes in v5:
time: 34.4 us; the launch traced here: 34.1 us
  starting transfers between devices  12.7 us (37%)
  blocking collectives  11.3 us (33%)
  Pallas kernels  6.66 us (19%)
  waiting for transfers between devices  2.74 us (8%)
  between operations  0.68 us (2%)
    all_to_all x1, blocking collectives, shards(): lax.all_to_all(send.reshape(32, BACK, 1, LANES), ('gx', 'gy'), 0, 0, tile...  11.3 us
    all_to_all x1, starting transfers between devices, shards(): lax.all_to_all(send.reshape(32, SENT, 1, LANES), ('gx', 'gy'), 0, 0, tile...  7.3 us
    ppermute x1, starting transfers between devices, shards(): pair = lax.ppermute(pair, 'gx', both(0))  4.45 us
    all_to_all x1, waiting for transfers between devices, shards(): lax.all_to_all(send.reshape(32, SENT, 1, LANES), ('gx', 'gy'), 0, 0, tile...  2.73 us
    pallas_call x1, Pallas kernels, shards(): pl.pallas_call(lambda *refs: slab_kernel(amplitude, *refs), out_shape=[vm...  2.53 us
    pallas_call x1, Pallas kernels, shards(): pl.pallas_call(interior_kernel, out_shape=[vmem(4, *cells), vmem(2, 4, 2,...  2.1 us
    pallas_call x1, Pallas kernels, shards(): pl.pallas_call(lambda *refs: final_kernel(scale, *refs), out_shape=[f32(5...  1.05 us
    pallas_call x1, Pallas kernels, shards(): pl.pallas_call(pencil_kernel, out_shape=[vmem(32 * BACK, LANES)] + [vmem(...  0.99 us
  transfers between devices with their start and end apart: 4, of which 1 were waited for; matrix products, arithmetic and copies ran while one was open for 0% of the time, Pallas kernels for 6%

profile of v5, /device:TPU:0, one launch (start us, length us, event | category | flops | bytes accessed | tf_op | source)
XLA Modules:
  0.0 34.1 jit_solution(4761180047568392945)
XLA Ops:
  0.6 2.5 %slab.1 = (f32[480,128]{1,0:T(8,128)}, f32[5,8,128]{2,1,0:T(8,128)S(1)}, f32[5,8,128]{2,1,0:T(8,128)S(1)}, f32[8,8,128]{2,1,0:T(8,128)S(1)}) custom-call(f32[8,32,32]{2,1,0:T(8,128)} %density.1, f32[3,8,32,32]{3,2,1,0:T(8,128)} %momentum.1, f32[8,32,32]{2,1,0:T(8,128)} %energy.1, s32[1,64]{1,0:T(1,128)} %bitcast.14, s32[1,64]{1,0:T(1,128)} %bitcast.15, ...), custom_call_target="tpu_custom_call" | custom-call | tf_op jit(solution)/shard_map/slab/pallas_call | solution.py:707
  3.2 7.3 %all-to-all-start = ((f32[32,15,1,128]{3,2,1,0:T(1,128)}), f32[32,15,1,128]{3,2,1,0:T(1,128)S(1)}, u32[]{:S(2)}, u32[]{:S(2)}) async-start(f32[32,15,1,128]{3,2,1,0:T(1,128)} %bitcast.4), calls=%async_computation | async-start | bytes 491520 | tf_op jit(solution)/shard_map/all_to_all | solution.py:720
  10.5 0.3 collective-permute-start
  10.8 0.7 %collective-permute-start.1 = (f32[5,8,128]{2,1,0:T(8,128)S(1)}, f32[5,8,128]{2,1,0:T(8,128)S(1)}, u32[]{:S(2)}, u32[]{:S(2)}) collective-permute-start(f32[5,8,128]{2,1,0:T(8,128)S(1)} %get-tuple-element.25), channel_id=1, source_target_pairs={{2,4},{4,2},{6,8},{8,6},{10,12},{12,10},{14,16},{16,14},{18,20},{2... | collective-permute-start | bytes 61448 | tf_op jit(solution)/shard_map/ppermute | solution.py:722
  11.4 4.5 %collective-permute-start.2 = (f32[5,8,128]{2,1,0:T(8,128)S(1)}, f32[5,8,128]{2,1,0:T(8,128)S(1)}, u32[]{:S(2)}, u32[]{:S(2)}) collective-permute-start(f32[5,8,128]{2,1,0:T(8,128)S(1)} %get-tuple-element.26), channel_id=1, source_target_pairs={{0,2},{2,0},{4,6},{6,4},{8,10},{10,8},{12,14},{14,12},{16,18},{18,... | collective-permute-start | bytes 61448 | tf_op jit(solution)/shard_map/ppermute | solution.py:723
  15.9 0.0 collective-permute-done.edge
  15.9 2.1 %interior.1 = (f32[4,8,8,128]{3,2,1,0:T(8,128)S(1)}, f32[2,4,2,8,128]{4,3,2,1,0:T(8,128)S(1)}, f32[4,8,8,128]{3,2,1,0:T(8,128)S(1)}, f32[9,2,8,128]{3,2,1,0:T(8,...) custom-call(f32[8,32,32]{2,1,0:T(8,128)} %density.1, ...), custom_call_target="tpu_custom_call" | custom-call | flops 10000000 | bytes 2000000 | tf_op jit(solution)/shard_map/interior/pallas_call | solution.py:725
  18.0 0.0 collective-permute-done.1.far
  18.0 0.0 collective-permute-done.2.pair
  18.0 2.7 %all-to-all-done = f32[32,15,1,128]{3,2,1,0:T(1,128)S(1)} async-done(((f32[32,15,1,128]{3,2,1,0:T(1,128)}), f32[32,15,1,128]{3,2,1,0:T(1,128)S(1)}, u32[]{:S(2)}, u32[]{:S(2)}) %all-to-all-start) | async-done | bytes 245792 | tf_op jit(solution)/shard_map/all_to_all | solution.py:720
  20.8 1.0 %pencil.1 = (f32[416,128]{1,0:T(8,128)S(1)}, f32[2,4,8,128]{3,2,1,0:T(8,128)S(1)}, f32[2,4,8,128]{3,2,1,0:T(8,128)S(1)}, f32[2,4,8,128]{3,2,1,0:T(8,128)S(1)}) custom-call(f32[480,128]{1,0:T(8,128)S(1)} %bitcast.9, bf16[2,128,128]{2,1,0:T(8,128)(2,1)S(1)} %get-tuple-element.20.matrix, f32[9,2,8,128]{3,2,1,0:T(8,128)S(1)} %get-tuple-element.21.ends, ...), custom_call_target="tpu_custom_call" | custom-call | tf_op jit(solution)/shard_map/pencil/pallas_call | solution.py:749
  21.7 11.3 %all_to_all.10 = f32[32,13,1,128]{3,2,1,0:T(1,128)S(1)} all-to-all(f32[32,13,1,128]{3,2,1,0:T(1,128)S(1)} %bitcast.11), channel_id=1, replica_groups=mesh['gx'=16,'gy'=2] {'gx','gy'}, dimensions={0} | all-to-all | bytes 425984 | tf_op jit(solution)/shard_map/all_to_all | solution.py:758
  33.1 1.0 %final.1 = (f32[5,8,32,32]{3,2,1,0:T(8,128)}, f32[64,64]{1,0:T(8,128)}) custom-call(f32[416,128]{1,0:T(8,128)S(1)} %bitcast.10, f32[4,8,8,128]{3,2,1,0:T(8,128)S(1)} %get-tuple-element.28.refs_1_, f32[2,4,2,8,128]{4,3,2,1,0:T(8,128)S(1)} %get-tuple-element.29.refs_2_, f32[4,8,8,128]{3,2,1,0:T(8,128)S(1)} %get-tuple-element.30.refs_3_, ...), custom_call_target="tpu_custom_call" | custom-call | tf_op jit(solution)/shard_map/final/pallas_call | solution.py:760
Async XLA Ops:
  3.2 17.6 %all-to-all-start = ((f32[32,15,1,128]{3,2,1,0:T(1,128)}), f32[32,15,1,128]{3,2,1,0:T(1,128)S(1)}, u32[]{:S(2)}, u32[]{:S(2)}) async-start(f32[32,15,1,128]{3,2,1,0:T(1,128)} %bitcast.4), calls=%async_computation | async-start | bytes 491520 | tf_op jit(solution)/shard_map/all_to_all | solution.py:720
  10.5 5.4 %collective-permute-start = (f32[8,8,128]{2,1,0:T(8,128)S(1)}, f32[8,8,128]{2,1,0:T(8,128)S(1)}, u32[]{:S(2)}, u32[]{:S(2)}) collective-permute-start(f32[8,8,128]{2,1,0:T(8,128)S(1)} %get-tuple-element.19), channel_id=1, source_target_pairs={{0,1},{1,0},{2,3},{3,2},{4,5},{5,4},{6,7},{7,6},{8,9},{9,8},{10,11... | collective-permute-start | bytes 98312 | tf_op jit(solution)/shard_map/ppermute | solution.py:724
  10.8 7.2 %collective-permute-start.1 = (f32[5,8,128]{2,1,0:T(8,128)S(1)}, f32[5,8,128]{2,1,0:T(8,128)S(1)}, u32[]{:S(2)}, u32[]{:S(2)}) collective-permute-start(f32[5,8,128]{2,1,0:T(8,128)S(1)} %get-tuple-element.25), channel_id=1, source_target_pairs={{2,4},{4,2},{6,8},{8,6},{10,12},{12,10},{14,16},{16,14},{18,20},{2... | collective-permute-start | bytes 61448 | tf_op jit(solution)/shard_map/ppermute | solution.py:722
  11.4 6.6 %collective-permute-start.2 = (f32[5,8,128]{2,1,0:T(8,128)S(1)}, f32[5,8,128]{2,1,0:T(8,128)S(1)}, u32[]{:S(2)}, u32[]{:S(2)}) collective-permute-start(f32[5,8,128]{2,1,0:T(8,128)S(1)} %get-tuple-element.26), channel_id=1, source_target_pairs={{0,2},{2,0},{4,6},{6,4},{8,10},{10,8},{12,14},{14,12},{16,18},{18,... | collective-permute-start | bytes 61448 | tf_op jit(solution)/shard_map/ppermute | solution.py:723

commit v6 on v5

--- a/solution.py
+++ b/solution.py
@@ -196,7 +196,7 @@
 
 
 LANES = 128
-SENT = 15
+SENT = 14
 BACK = 13
 HALF_STEP = 0.5 * TIME_STEP
 
@@ -311,8 +311,12 @@
             side = jnp.where(lane2 % 32 == x, pltpu.roll(value[x], shift + x, 1), side)
         edge_out[i] = side
         sides.append(side)
-    energy_side = roll(sides[4], 8, 1)
-    sides = [jnp.where(lane2 % 32 < 8, sides[0], energy_side)] + sides[1:4]
+    across = jnp.zeros((8, LANES), jnp.float32)
+    for f in range(5):
+        mine = (lane2 % 32 >= 6 * f) & (lane2 % 32 < 6 * f + 6)
+        across = jnp.where(mine, roll(sides[f], 6 * f - 1, 1), across)
+    corner = lane2 % 32 == jnp.where(first_core, 31, 0)
+    end_rows = [[jnp.where(corner, q[f][x], flux_x[f][x]) for f in range(5)] for x in (7, 0)]
 
     pick = lambda a: jnp.where(first_core, a[:, :32], a[:, 32:])
     strength = strengths[...] * amplitude
@@ -324,12 +328,12 @@
     eddy_rest = jnp.broadcast_to(jnp.concatenate([eddies[4]] * 4, axis=1), (8, LANES))
     cells = regrouped(partial[:4])
     energies = [regrouped([partial[4][4 * a + b] for b in range(4)]) for a in range(2)]
-    faces = [regrouped([flux_x[f][x] for f in range(4)]) for x in (7, 0)]
+    faces = [regrouped(a[:4]) for a in end_rows]
     blank = jnp.zeros_like(eddy_rest)
-    sides, ends = regrouped(sides), regrouped([blank, flux_x[4][7], flux_x[4][0], blank])
+    ends = regrouped([blank, end_rows[0][4], end_rows[1][4], across])
     for k in range(4):
         rows = [cells[k][x] for x in range(8)] + [e[k] for e in energies] + [a[k] for a in faces]
-        rows += [sides[k], eddy_row, jnp.where(lane2 < 32, eddy_rest, ends[k])]
+        rows += [eddy_row, jnp.where(lane2 < 32, eddy_rest, ends[k])]
         for r, value in enumerate(rows):
             send[pl.ds(8 * SENT * k + r, 8, stride=SENT), :] = value
 
@@ -498,8 +502,8 @@
             out = moved if out is None else jnp.where(lane // 32 == j, moved, out)
         return out
 
-    centre_y, centre_z = side_by_side(13, 0), side_by_side(13, 1)
-    strength = [side_by_side(13, 2), side_by_side(13, 3), side_by_side(14, 0)]
+    centre_y, centre_z = side_by_side(12, 0), side_by_side(12, 1)
+    strength = [side_by_side(12, 2), side_by_side(12, 3), side_by_side(13, 0)]
     strength = [a * peak for a in strength]
     @pl.when(slab == 0)
     def _():
@@ -543,18 +547,36 @@
     row16 = iota((16, LANES), 0)
     lane16 = iota((16, LANES), 1)
     chunk_row = lambda r, h: received[pl.ds(SENT * h + r, 16, stride=2 * SENT), :]
+    edges = (31, 0)
+    ends_a, ends_e, corners = [], [], []
+    for h in range(2):
+        rest = chunk_row(13, h)
+        for end in range(2):
+            a, e = chunk_row(10 + end, h), roll(rest, -32 * (1 + end), 1)
+            q = [roll(a, -32 * f, 1) for f in range(4)] + [e]
+            vel, pressure = velocity_pressure(q)
+            flux = euler_flux(q, vel, pressure, 0)
+            for f in range(4):
+                a = jnp.where(lane16 == 32 * f + edges[h], roll(flux[f], 32 * f, 1), a)
+            ends_a.append(a)
+            ends_e.append(jnp.where(lane16 == edges[h], flux[4], e))
+            flux = euler_flux(q, vel, pressure, 1)
+            four = flux[0]
+            for f in range(1, 4):
+                four = jnp.where(lane16 // 32 == f, roll(flux[f], 32 * f, 1), four)
+            corners.append((four, flux[4]))
     columns, energy_columns = [], []
     for h in range(2):
-        target = 31 if h == 0 else 0
+        target, other = edges[h], edges[1 - h]
         side = -HALF_STEP if h == 0 else HALF_STEP
-        across = side * chunk_row(12, 1 - h)
-        both_ends = chunk_row(14, h)
-        last_a, first_a = chunk_row(10, h), chunk_row(11, h)
-        last_e, first_e = roll(both_ends, -32, 1), roll(both_ends, -64, 1)
-        before_a = jnp.where(row16 == 0, 0.0, roll(last_a, 1, 0))
-        before_e = jnp.where(row16 == 0, 0.0, roll(last_e, 1, 0))
-        after_a = jnp.where(row16 == 15, 0.0, roll(first_a, -1, 0))
-        after_e = jnp.where(row16 == 15, 0.0, roll(first_e, -1, 0))
+        across = chunk_row(13, 1 - h)
+        across_a = roll(across, -96, 1)
+        for f in range(1, 4):
+            across_a = jnp.where(lane16 // 32 == f, roll(across, 26 * f - 96, 1), across_a)
+        before_a = jnp.where(row16 == 0, 0.0, roll(ends_a[2 * h], 1, 0))
+        before_e = jnp.where(row16 == 0, 0.0, roll(ends_e[2 * h], 1, 0))
+        after_a = jnp.where(row16 == 15, 0.0, roll(ends_a[2 * h + 1], -1, 0))
+        after_e = jnp.where(row16 == 15, 0.0, roll(ends_e[2 * h + 1], -1, 0))
         for r in range(8):
             a = chunk_row(r, h)
             e = roll(chunk_row(8 + r // 4, h), -32 * (r % 4), 1)
@@ -562,8 +584,14 @@
                 a, e = a + HALF_STEP * before_a, e + HALF_STEP * before_e
             if r == 7:
                 a, e = a - HALF_STEP * after_a, e - HALF_STEP * after_e
-            a = jnp.where(lane16 % 32 == target, a + roll(across, target - r, 1), a)
-            e = jnp.where(lane16 == target, e + roll(across, target - r - 8, 1), e)
+            if r in (0, 7):
+                moved_a, moved_e = corners[2 * (1 - h) + (1 if r == 0 else 0)]
+                shift_a, shift_e = target - other, target - other
+            else:
+                moved_a, moved_e = across_a, across
+                shift_a, shift_e = target - (r - 1), target - (120 + r - 1)
+            a = jnp.where(lane16 % 32 == target, a + side * roll(moved_a, shift_a, 1), a)
+            e = jnp.where(lane16 == target, e + side * roll(moved_e, shift_e, 1), e)
             columns.append(a)
             energy_columns.append(roll(e, 32 * h, 1))
     joined = [jnp.where(lane16 < 32, energy_columns[r], energy_columns[8 + r]) for r in range(8)]

time: 34.4 us -> 34.3 us (level)
  waiting for transfers between devices: 2.74 us -> 2.27 us
    all_to_all x1, waiting for transfers between devices: 2.73 us -> 2.27 us  [shards(): lax.all_to_all(send.reshape(32, SENT, 1, LANES), ('gx', 'gy'), 0, 0, tile...]
where the time goes in v6:
time: 34.3 us; the launch traced here: 34 us
  starting transfers between devices  12.7 us (37%)
  blocking collectives  11.6 us (34%)
  Pallas kernels  6.8 us (20%)
  waiting for transfers between devices  2.27 us (7%)
  between operations  0.68 us (2%)
    all_to_all x1, blocking collectives, shards(): lax.all_to_all(send.reshape(32, BACK, 1, LANES), ('gx', 'gy'), 0, 0, tile...  11.6 us
    all_to_all x1, starting transfers between devices, shards(): lax.all_to_all(send.reshape(32, SENT, 1, LANES), ('gx', 'gy'), 0, 0, tile...  7.3 us
    ppermute x1, starting transfers between devices, shards(): pair = lax.ppermute(pair, 'gx', both(0))  4.45 us
    pallas_call x1, Pallas kernels, shards(): pl.pallas_call(lambda *refs: slab_kernel(amplitude, *refs), out_shape=[vm...  2.54 us
    all_to_all x1, waiting for transfers between devices, shards(): lax.all_to_all(send.reshape(32, SENT, 1, LANES), ('gx', 'gy'), 0, 0, tile...  2.27 us
    pallas_call x1, Pallas kernels, shards(): pl.pallas_call(interior_kernel, out_shape=[vmem(4, *cells), vmem(2, 4, 2,...  2.1 us
    pallas_call x1, Pallas kernels, shards(): pl.pallas_call(pencil_kernel, out_shape=[vmem(32 * BACK, LANES)] + [vmem(...  1.11 us
    pallas_call x1, Pallas kernels, shards(): pl.pallas_call(lambda *refs: final_kernel(scale, *refs), out_shape=[f32(5...  1.05 us
  transfers between devices with their start and end apart: 4, of which 1 were waited for; matrix products, arithmetic and copies ran while one was open for 0% of the time, Pallas kernels for 6%

profile of v6, /device:TPU:0, one launch (start us, length us, event | category | flops | bytes accessed | tf_op | source)
XLA Modules:
  0.0 34.0 jit_solution(10031874153995235693)
XLA Ops:
  0.6 2.5 %slab.1 = (f32[448,128]{1,0:T(8,128)}, f32[5,8,128]{2,1,0:T(8,128)S(1)}, f32[5,8,128]{2,1,0:T(8,128)S(1)}, f32[8,8,128]{2,1,0:T(8,128)S(1)}) custom-call(f32[8,32,32]{2,1,0:T(8,128)} %density.1, f32[3,8,32,32]{3,2,1,0:T(8,128)} %momentum.1, f32[8,32,32]{2,1,0:T(8,128)} %energy.1, s32[1,64]{1,0:T(1,128)} %bitcast.14, s32[1,64]{1,0:T(1,128)} %bitcast.15, ...), custom_call_target="tpu_custom_call" | custom-call | tf_op jit(solution)/shard_map/slab/pallas_call | solution.py:735
  3.2 7.3 %all-to-all-start = ((f32[32,14,1,128]{3,2,1,0:T(1,128)}), f32[32,14,1,128]{3,2,1,0:T(1,128)S(1)}, u32[]{:S(2)}, u32[]{:S(2)}) async-start(f32[32,14,1,128]{3,2,1,0:T(1,128)} %bitcast.4), calls=%async_computation | async-start | bytes 458752 | tf_op jit(solution)/shard_map/all_to_all | solution.py:748
  10.5 0.3 collective-permute-start
  10.8 0.7 %collective-permute-start.1 = (f32[5,8,128]{2,1,0:T(8,128)S(1)}, f32[5,8,128]{2,1,0:T(8,128)S(1)}, u32[]{:S(2)}, u32[]{:S(2)}) collective-permute-start(f32[5,8,128]{2,1,0:T(8,128)S(1)} %get-tuple-element.25), channel_id=1, source_target_pairs={{2,4},{4,2},{6,8},{8,6},{10,12},{12,10},{14,16},{16,14},{18,20},{2... | collective-permute-start | bytes 61448 | tf_op jit(solution)/shard_map/ppermute | solution.py:750
  11.4 4.5 %collective-permute-start.2 = (f32[5,8,128]{2,1,0:T(8,128)S(1)}, f32[5,8,128]{2,1,0:T(8,128)S(1)}, u32[]{:S(2)}, u32[]{:S(2)}) collective-permute-start(f32[5,8,128]{2,1,0:T(8,128)S(1)} %get-tuple-element.26), channel_id=1, source_target_pairs={{0,2},{2,0},{4,6},{6,4},{8,10},{10,8},{12,14},{14,12},{16,18},{18,... | collective-permute-start | bytes 61448 | tf_op jit(solution)/shard_map/ppermute | solution.py:751
  15.9 0.0 collective-permute-done.edge
  15.9 2.1 %interior.1 = (f32[4,8,8,128]{3,2,1,0:T(8,128)S(1)}, f32[2,4,2,8,128]{4,3,2,1,0:T(8,128)S(1)}, f32[4,8,8,128]{3,2,1,0:T(8,128)S(1)}, f32[9,2,8,128]{3,2,1,0:T(8,...) custom-call(f32[8,32,32]{2,1,0:T(8,128)} %density.1, ...), custom_call_target="tpu_custom_call" | custom-call | flops 10000000 | bytes 2000000 | tf_op jit(solution)/shard_map/interior/pallas_call | solution.py:753
  18.0 0.0 collective-permute-done.1.far
  18.0 0.0 collective-permute-done.2.pair
  18.0 2.3 %all-to-all-done = f32[32,14,1,128]{3,2,1,0:T(1,128)S(1)} async-done(((f32[32,14,1,128]{3,2,1,0:T(1,128)}), f32[32,14,1,128]{3,2,1,0:T(1,128)S(1)}, u32[]{:S(2)}, u32[]{:S(2)}) %all-to-all-start) | async-done | bytes 229408 | tf_op jit(solution)/shard_map/all_to_all | solution.py:748
  20.3 1.1 %pencil.1 = (f32[416,128]{1,0:T(8,128)S(1)}, f32[2,4,8,128]{3,2,1,0:T(8,128)S(1)}, f32[2,4,8,128]{3,2,1,0:T(8,128)S(1)}, f32[2,4,8,128]{3,2,1,0:T(8,128)S(1)}) custom-call(f32[448,128]{1,0:T(8,128)S(1)} %bitcast.9, bf16[2,128,128]{2,1,0:T(8,128)(2,1)S(1)} %get-tuple-element.20.matrix, f32[9,2,8,128]{3,2,1,0:T(8,128)S(1)} %get-tuple-element.21.ends, ...), custom_call_target="tpu_custom_call" | custom-call | tf_op jit(solution)/shard_map/pencil/pallas_call | solution.py:777
  21.4 11.6 %all_to_all.10 = f32[32,13,1,128]{3,2,1,0:T(1,128)S(1)} all-to-all(f32[32,13,1,128]{3,2,1,0:T(1,128)S(1)} %bitcast.11), channel_id=1, replica_groups=mesh['gx'=16,'gy'=2] {'gx','gy'}, dimensions={0} | all-to-all | bytes 425984 | tf_op jit(solution)/shard_map/all_to_all | solution.py:786
  33.0 1.0 %final.1 = (f32[5,8,32,32]{3,2,1,0:T(8,128)}, f32[64,64]{1,0:T(8,128)}) custom-call(f32[416,128]{1,0:T(8,128)S(1)} %bitcast.10, f32[4,8,8,128]{3,2,1,0:T(8,128)S(1)} %get-tuple-element.28.refs_1_, f32[2,4,2,8,128]{4,3,2,1,0:T(8,128)S(1)} %get-tuple-element.29.refs_2_, f32[4,8,8,128]{3,2,1,0:T(8,128)S(1)} %get-tuple-element.30.refs_3_, ...), custom_call_target="tpu_custom_call" | custom-call | tf_op jit(solution)/shard_map/final/pallas_call | solution.py:788
Async XLA Ops:
  3.2 17.1 %all-to-all-start = ((f32[32,14,1,128]{3,2,1,0:T(1,128)}), f32[32,14,1,128]{3,2,1,0:T(1,128)S(1)}, u32[]{:S(2)}, u32[]{:S(2)}) async-start(f32[32,14,1,128]{3,2,1,0:T(1,128)} %bitcast.4), calls=%async_computation | async-start | bytes 458752 | tf_op jit(solution)/shard_map/all_to_all | solution.py:748
  10.5 5.4 %collective-permute-start = (f32[8,8,128]{2,1,0:T(8,128)S(1)}, f32[8,8,128]{2,1,0:T(8,128)S(1)}, u32[]{:S(2)}, u32[]{:S(2)}) collective-permute-start(f32[8,8,128]{2,1,0:T(8,128)S(1)} %get-tuple-element.19), channel_id=1, source_target_pairs={{0,1},{1,0},{2,3},{3,2},{4,5},{5,4},{6,7},{7,6},{8,9},{9,8},{10,11... | collective-permute-start | bytes 98312 | tf_op jit(solution)/shard_map/ppermute | solution.py:752
  10.8 7.2 %collective-permute-start.1 = (f32[5,8,128]{2,1,0:T(8,128)S(1)}, f32[5,8,128]{2,1,0:T(8,128)S(1)}, u32[]{:S(2)}, u32[]{:S(2)}) collective-permute-start(f32[5,8,128]{2,1,0:T(8,128)S(1)} %get-tuple-element.25), channel_id=1, source_target_pairs={{2,4},{4,2},{6,8},{8,6},{10,12},{12,10},{14,16},{16,14},{18,20},{2... | collective-permute-start | bytes 61448 | tf_op jit(solution)/shard_map/ppermute | solution.py:750
  11.4 6.6 %collective-permute-start.2 = (f32[5,8,128]{2,1,0:T(8,128)S(1)}, f32[5,8,128]{2,1,0:T(8,128)S(1)}, u32[]{:S(2)}, u32[]{:S(2)}) collective-permute-start(f32[5,8,128]{2,1,0:T(8,128)S(1)} %get-tuple-element.26), channel_id=1, source_target_pairs={{0,2},{2,0},{4,6},{6,4},{8,10},{10,8},{12,14},{14,12},{16,18},{18,... | collective-permute-start | bytes 61448 | tf_op jit(solution)/shard_map/ppermute | solution.py:751
